TPU v7x, 1024 devices: a whole 8x8x8 slice. The times are simulated.
1024 devices in a mesh: ctx: 128 (over z, y, core), head: 4 (over x_hi), batch: 2 (over x_lo).
Axes of the slice: x: 8 (x_hi: 4, x_lo: 2; x = x_hi * 2 + x_lo), y: 8, z: 8, core: 2. Of those that a mesh axis runs over, the one named last changes fastest.
Arguments:
- queries: bfloat16 [32768, 4096], P(('batch', 'ctx'), 'head'), parts along dimension 0, may hold values from -200 to 200
- key_rows: bfloat16 [32768, 1024], P(('batch', 'ctx'), 'head'), parts along dimension 0, may hold values from -7 to 7
- values: bfloat16 [32768, 1024], P(('batch', 'ctx'), 'head'), parts along dimension 0, may hold values from -6 to 6
- doc_lengths: int32 [128], P('batch'), parts along dimension 0, may hold values from 1 to 1920, 16384 in all
- out_weight: bfloat16 [4096, 4096], P('head'), may hold values from -0.125 to 0.125
Outputs:
- layer_out: bfloat16 [32768, 4096], P(('batch', 'ctx'), 'head'), parts along dimension 0
There are 2 independent parts, one for each index of `batch`. A program takes and returns all parts, laid end to end along the dimension named above; an argument that names none is the same for every part. Nothing has to cross between parts.
Inputs may be any that keep to these rules, and one draw needn't show every extreme that they name: `doc_lengths`: the lengths sum to 16384, and the longest document has exactly 1920 tokens.
All inputs are finite; a program needn't handle non-finite values.
Results may differ from a plain program's by a relative error of at most 0.0052.
Values may be sent and summed in bfloat16 or wider, within the bound.
No kernel may reach another device: no remote copies, remote signals or barrier semaphores. Data moves between devices by JAX's collectives and lax.ppermute only.
A program may use at most 32 MiB of HBM per device.

v0:
```python
import jax
import jax.numpy as jnp
from jax import lax
from jax.sharding import PartitionSpec as P

HEADS = 32
KV_HEADS = 8
HEAD_DIM = 128


def shifted(value, axis, by):
    devices = lax.axis_size(axis)
    pairs = [(i, i + by) for i in range(devices) if 0 <= i + by < devices]
    return lax.ppermute(value, axis, pairs)


def doc_ids(doc_ends, positions):
    return jnp.sum((doc_ends[None, :] <= positions[:, None]).astype(jnp.int32), axis=1)


def per_device(queries, key_rows, values, doc_lengths, out_weight):
    ctx_size = lax.axis_size("ctx")
    reach_devs = min(16, ctx_size)
    my_index = lax.axis_index("ctx")
    tok_rows = queries.shape[0]
    kv_width = key_rows.shape[1]
    local_heads = kv_width // HEAD_DIM
    group_size = HEADS // KV_HEADS
    score_scale = HEAD_DIM ** (-0.5)
    empty_rows = jnp.zeros((reach_devs * tok_rows, kv_width), jnp.bfloat16)
    last_offset = (reach_devs - 1) * tok_rows
    start_keys = lax.dynamic_update_slice_in_dim(empty_rows, key_rows, last_offset, 0)
    start_values = lax.dynamic_update_slice_in_dim(empty_rows, values, last_offset, 0)

    def advance(step_index, carry):
        moving_keys, moving_values, kept_keys, kept_values = carry
        moving_keys, moving_values = shifted((moving_keys, moving_values), "ctx", 1)
        offset = (reach_devs - 2 - step_index) * tok_rows
        kept_keys = lax.dynamic_update_slice_in_dim(kept_keys, moving_keys, offset, 0)
        kept_values = lax.dynamic_update_slice_in_dim(kept_values, moving_values, offset, 0)
        return (moving_keys, moving_values, kept_keys, kept_values)

    final_state = lax.fori_loop(
        0, reach_devs - 1, advance, (key_rows, values, start_keys, start_values)
    )
    held_keys = final_state[2]
    held_values = final_state[3]
    doc_ends = jnp.cumsum(doc_lengths)
    query_pos = my_index * tok_rows + jnp.arange(tok_rows, dtype=jnp.int32)
    key_pos = (my_index - reach_devs + 1) * tok_rows + jnp.arange(
        reach_devs * tok_rows, dtype=jnp.int32
    )
    query_docs = doc_ids(doc_ends, query_pos)
    key_docs = jnp.where(key_pos >= 0, doc_ids(doc_ends, key_pos), -1)
    allowed = (key_docs[None, :] == query_docs[:, None]) & (key_pos[None, :] <= query_pos[:, None])
    pieces = []
    for head_pair in range(local_heads):
        query_block = queries[
            :, head_pair * group_size * HEAD_DIM : (head_pair + 1) * group_size * HEAD_DIM
        ]
        query_block = query_block.reshape(tok_rows, group_size, HEAD_DIM)
        key_block = held_keys[:, head_pair * HEAD_DIM : (head_pair + 1) * HEAD_DIM]
        value_block = held_values[:, head_pair * HEAD_DIM : (head_pair + 1) * HEAD_DIM]
        scores = (
            jnp.einsum("tgd,sd->gts", query_block, key_block, preferred_element_type=jnp.float32)
            * score_scale
        )
        scores = jnp.where(allowed[None], scores, -1e30)
        row_peak = jnp.max(scores, axis=2, keepdims=True)
        weights = jnp.exp(scores - row_peak)
        row_total = jnp.sum(weights, axis=2, keepdims=True)
        mixed_out = jnp.einsum(
            "gts,sd->gtd",
            weights.astype(jnp.bfloat16),
            value_block,
            preferred_element_type=jnp.float32,
        )
        mixed_out = mixed_out / row_total
        pieces.append(
            jnp.transpose(mixed_out, (1, 0, 2))
            .astype(jnp.bfloat16)
            .reshape(tok_rows, group_size * HEAD_DIM)
        )
    attended = jnp.concatenate(pieces, axis=1)
    partial_out = jnp.dot(attended, out_weight, preferred_element_type=jnp.float32)
    return lax.psum_scatter(partial_out, "head", scatter_dimension=1, tiled=True).astype(
        jnp.bfloat16
    )


def solution(mesh):
    return jax.shard_map(
        per_device,
        mesh=mesh,
        in_specs=(
            P(("batch", "ctx"), "head"),
            P(("batch", "ctx"), "head"),
            P(("batch", "ctx"), "head"),
            P("batch"),
            P("head", None),
        ),
        out_specs=P(("batch", "ctx"), "head"),
        check_vma=False,
    )
```

profile of v0, /device:TPU:16, one launch (start us, length us, event | category | flops | bytes accessed | tf_op | source)
XLA Modules:
  0.0 251.0 jit_solution(17809019590138943153)
XLA Ops:
  10.8 126.3 %while.19 = (s32[]{:T(128)}, bf16[128,256]{1,0:T(8,128)(2,1)S(1)}, bf16[128,256]{1,0:T(8,128)(2,1)S(1)}, bf16[2048,256]{1,0:T(8,128)(2,1)S(1)}, bf16[2048,256]{1...) while((s32[]{:T(128)}, bf16[128,256]{1,0:T(8,128)(2,1)S(1)}, ...), condition=%wide.region_4.5_spmd, body=%wide.region_3.4_spmd.sunk | while | flops 7 | bytes 1048823 | solution.py:43
  12.8 3.7 %collective-permute-start = (bf16[128,256]{1,0:T(8,128)(2,1)S(1)}, bf16[128,256]{1,0:T(8,128)(2,1)S(1)}, u32[]{:S(2)}, u32[]{:S(2)}) collective-permute-start(bf16[128,256]{1,0:T(8,128)(2,1)S(1)} %get-tuple-element.160), channel_id=1, source_target_pairs={{0,8},{8,16},{16,24},{24,32},{32,40},{40,48},{48,56},{56,64},{64,7... | collective-permute-start | bytes 196616 | tf_op jit(solution)/shard_map/while/body/eval_jaxpr/ppermute | solution.py:14
  20.3 3.7 %collective-permute-start = (bf16[128,256]{1,0:T(8,128)(2,1)S(1)}, bf16[128,256]{1,0:T(8,128)(2,1)S(1)}, u32[]{:S(2)}, u32[]{:S(2)}) collective-permute-start(bf16[128,256]{1,0:T(8,128)(2,1)S(1)} %get-tuple-element.160), channel_id=1, source_target_pairs={{0,8},{8,16},{16,24},{24,32},{32,40},{40,48},{48,56},{56,64},{64,7... | collective-permute-start | bytes 196616 | tf_op jit(solution)/shard_map/while/body/eval_jaxpr/ppermute | solution.py:14
  24.1 7.1 %collective-permute-done.1 = bf16[128,256]{1,0:T(8,128)(2,1)S(1)} collective-permute-done((bf16[128,256]{1,0:T(8,128)(2,1)S(1)}, bf16[128,256]{1,0:T(8,128)(2,1)S(1)}, u32[]{:S(2)}, u32[]{:S(2)}) %collective-permute-start.1) | collective-permute-done | bytes 65568 | tf_op jit(solution)/shard_map/while/body/eval_jaxpr/ppermute | solution.py:14
  31.2 1.9 collective-permute-done
  38.7 1.9 collective-permute-done
  46.3 1.9 collective-permute-done
  53.9 1.9 collective-permute-done
  61.4 1.9 collective-permute-done
  69.0 1.9 collective-permute-done
  80.5 3.0 %collective-permute-start = (bf16[128,256]{1,0:T(8,128)(2,1)S(1)}, bf16[128,256]{1,0:T(8,128)(2,1)S(1)}, u32[]{:S(2)}, u32[]{:S(2)}) collective-permute-start(bf16[128,256]{1,0:T(8,128)(2,1)S(1)} %get-tuple-element.160), channel_id=1, source_target_pairs={{0,8},{8,16},{16,24},{24,32},{32,40},{40,48},{48,56},{56,64},{64,7... | collective-permute-start | bytes 196616 | tf_op jit(solution)/shard_map/while/body/eval_jaxpr/ppermute | solution.py:14
  88.0 4.2 %collective-permute-start = (bf16[128,256]{1,0:T(8,128)(2,1)S(1)}, bf16[128,256]{1,0:T(8,128)(2,1)S(1)}, u32[]{:S(2)}, u32[]{:S(2)}) collective-permute-start(bf16[128,256]{1,0:T(8,128)(2,1)S(1)} %get-tuple-element.160), channel_id=1, source_target_pairs={{0,8},{8,16},{16,24},{24,32},{32,40},{40,48},{48,56},{56,64},{64,7... | collective-permute-start | bytes 196616 | tf_op jit(solution)/shard_map/while/body/eval_jaxpr/ppermute | solution.py:14
  93.7 2.8 %collective-permute-start.1 = (bf16[128,256]{1,0:T(8,128)(2,1)S(1)}, bf16[128,256]{1,0:T(8,128)(2,1)S(1)}, u32[]{:S(2)}, u32[]{:S(2)}) collective-permute-start(bf16[128,256]{1,0:T(8,128)(2,1)S(1)} %get-tuple-element.161), channel_id=1, source_target_pairs={{0,8},{8,16},{16,24},{24,32},{32,40},{40,48},{48,56},{56,64},{64,7... | collective-permute-start | bytes 196616 | tf_op jit(solution)/shard_map/while/body/eval_jaxpr/ppermute | solution.py:14
  96.4 4.6 %collective-permute-start = (bf16[128,256]{1,0:T(8,128)(2,1)S(1)}, bf16[128,256]{1,0:T(8,128)(2,1)S(1)}, u32[]{:S(2)}, u32[]{:S(2)}) collective-permute-start(bf16[128,256]{1,0:T(8,128)(2,1)S(1)} %get-tuple-element.160), channel_id=1, source_target_pairs={{0,8},{8,16},{16,24},{24,32},{32,40},{40,48},{48,56},{56,64},{64,7... | collective-permute-start | bytes 196616 | tf_op jit(solution)/shard_map/while/body/eval_jaxpr/ppermute | solution.py:14
  102.1 3.1 %collective-permute-start.1 = (bf16[128,256]{1,0:T(8,128)(2,1)S(1)}, bf16[128,256]{1,0:T(8,128)(2,1)S(1)}, u32[]{:S(2)}, u32[]{:S(2)}) collective-permute-start(bf16[128,256]{1,0:T(8,128)(2,1)S(1)} %get-tuple-element.161), channel_id=1, source_target_pairs={{0,8},{8,16},{16,24},{24,32},{32,40},{40,48},{48,56},{56,64},{64,7... | collective-permute-start | bytes 196616 | tf_op jit(solution)/shard_map/while/body/eval_jaxpr/ppermute | solution.py:14
  105.2 4.6 %collective-permute-start = (bf16[128,256]{1,0:T(8,128)(2,1)S(1)}, bf16[128,256]{1,0:T(8,128)(2,1)S(1)}, u32[]{:S(2)}, u32[]{:S(2)}) collective-permute-start(bf16[128,256]{1,0:T(8,128)(2,1)S(1)} %get-tuple-element.160), channel_id=1, source_target_pairs={{0,8},{8,16},{16,24},{24,32},{32,40},{40,48},{48,56},{56,64},{64,7... | collective-permute-start | bytes 196616 | tf_op jit(solution)/shard_map/while/body/eval_jaxpr/ppermute | solution.py:14
  110.8 3.1 %collective-permute-start.1 = (bf16[128,256]{1,0:T(8,128)(2,1)S(1)}, bf16[128,256]{1,0:T(8,128)(2,1)S(1)}, u32[]{:S(2)}, u32[]{:S(2)}) collective-permute-start(bf16[128,256]{1,0:T(8,128)(2,1)S(1)} %get-tuple-element.161), channel_id=1, source_target_pairs={{0,8},{8,16},{16,24},{24,32},{32,40},{40,48},{48,56},{56,64},{64,7... | collective-permute-start | bytes 196616 | tf_op jit(solution)/shard_map/while/body/eval_jaxpr/ppermute | solution.py:14
  114.0 4.6 %collective-permute-start = (bf16[128,256]{1,0:T(8,128)(2,1)S(1)}, bf16[128,256]{1,0:T(8,128)(2,1)S(1)}, u32[]{:S(2)}, u32[]{:S(2)}) collective-permute-start(bf16[128,256]{1,0:T(8,128)(2,1)S(1)} %get-tuple-element.160), channel_id=1, source_target_pairs={{0,8},{8,16},{16,24},{24,32},{32,40},{40,48},{48,56},{56,64},{64,7... | collective-permute-start | bytes 196616 | tf_op jit(solution)/shard_map/while/body/eval_jaxpr/ppermute | solution.py:14
  119.6 3.1 %collective-permute-start.1 = (bf16[128,256]{1,0:T(8,128)(2,1)S(1)}, bf16[128,256]{1,0:T(8,128)(2,1)S(1)}, u32[]{:S(2)}, u32[]{:S(2)}) collective-permute-start(bf16[128,256]{1,0:T(8,128)(2,1)S(1)} %get-tuple-element.161), channel_id=1, source_target_pairs={{0,8},{8,16},{16,24},{24,32},{32,40},{40,48},{48,56},{56,64},{64,7... | collective-permute-start | bytes 196616 | tf_op jit(solution)/shard_map/while/body/eval_jaxpr/ppermute | solution.py:14
  122.8 4.6 %collective-permute-start = (bf16[128,256]{1,0:T(8,128)(2,1)S(1)}, bf16[128,256]{1,0:T(8,128)(2,1)S(1)}, u32[]{:S(2)}, u32[]{:S(2)}) collective-permute-start(bf16[128,256]{1,0:T(8,128)(2,1)S(1)} %get-tuple-element.160), channel_id=1, source_target_pairs={{0,8},{8,16},{16,24},{24,32},{32,40},{40,48},{48,56},{56,64},{64,7... | collective-permute-start | bytes 196616 | tf_op jit(solution)/shard_map/while/body/eval_jaxpr/ppermute | solution.py:14
  128.4 3.1 %collective-permute-start.1 = (bf16[128,256]{1,0:T(8,128)(2,1)S(1)}, bf16[128,256]{1,0:T(8,128)(2,1)S(1)}, u32[]{:S(2)}, u32[]{:S(2)}) collective-permute-start(bf16[128,256]{1,0:T(8,128)(2,1)S(1)} %get-tuple-element.161), channel_id=1, source_target_pairs={{0,8},{8,16},{16,24},{24,32},{32,40},{40,48},{48,56},{56,64},{64,7... | collective-permute-start | bytes 196616 | tf_op jit(solution)/shard_map/while/body/eval_jaxpr/ppermute | solution.py:14
  131.5 4.6 %collective-permute-start = (bf16[128,256]{1,0:T(8,128)(2,1)S(1)}, bf16[128,256]{1,0:T(8,128)(2,1)S(1)}, u32[]{:S(2)}, u32[]{:S(2)}) collective-permute-start(bf16[128,256]{1,0:T(8,128)(2,1)S(1)} %get-tuple-element.160), channel_id=1, source_target_pairs={{0,8},{8,16},{16,24},{24,32},{32,40},{40,48},{48,56},{56,64},{64,7... | collective-permute-start | bytes 196616 | tf_op jit(solution)/shard_map/while/body/eval_jaxpr/ppermute | solution.py:14
  144.4 2.6 %fusion.32 = f32[128,4096]{1,0:T(8,128)} fusion(bf16[1024,4096]{1,0:T(8,128)(2,1)S(1)} %bitcast.43, bf16[128,512]{0,1:T(8,128)(2,1)S(1)} %bitcast.45, bf16[128,512]{0,1:T(8,128)(2,1)S(1)} %bitcast.44), kind=kOutput, calls=%fused_computation.28 | convolution fusion | flops 1074266112 | bytes 10747904 | tf_op jit(solution)/shard_map/dot_general | solution.py:85
  147.1 95.3 %reduce-scatter.2.cloned.1.call-done = f32[128,1024]{1,0:T(8,128)} async-done(((f32[128,4096]{1,0:T(8,128)}), f32[128,1024]{1,0:T(8,128)}) %reduce-scatter.2.cloned.1.call-update) | async-done | bytes 524304 | tf_op jit(solution)/shard_map/reduce_scatter | solution.py:86
  (130 shorter events, 67.0 us)
Async XLA Ops:
  6.5 235.9 %reduce-scatter.2.cloned.1.call-start = ((), (), s32[]{:S(2)}) async-start(), calls=%async_computation.1 | async-start | bytes 2621440 | tf_op jit(solution)/shard_map/reduce_scatter | solution.py:86
  10.8 5.6 %collective-permute-start.1 = (bf16[128,256]{1,0:T(8,128)(2,1)S(1)}, bf16[128,256]{1,0:T(8,128)(2,1)S(1)}, u32[]{:S(2)}, u32[]{:S(2)}) collective-permute-start(bf16[128,256]{1,0:T(8,128)(2,1)S(1)} %get-tuple-element.161), channel_id=1, source_target_pairs={{0,8},{8,16},{16,24},{24,32},{32,40},{40,48},{48,56},{56,64},{64,7... | collective-permute-start | bytes 196616 | tf_op jit(solution)/shard_map/while/body/eval_jaxpr/ppermute | solution.py:14
  18.4 12.7 %collective-permute-start.1 = (bf16[128,256]{1,0:T(8,128)(2,1)S(1)}, bf16[128,256]{1,0:T(8,128)(2,1)S(1)}, u32[]{:S(2)}, u32[]{:S(2)}) collective-permute-start(bf16[128,256]{1,0:T(8,128)(2,1)S(1)} %get-tuple-element.161), channel_id=1, source_target_pairs={{0,8},{8,16},{16,24},{24,32},{32,40},{40,48},{48,56},{56,64},{64,7... | collective-permute-start | bytes 196616 | tf_op jit(solution)/shard_map/while/body/eval_jaxpr/ppermute | solution.py:14
  20.3 12.7 %collective-permute-start = (bf16[128,256]{1,0:T(8,128)(2,1)S(1)}, bf16[128,256]{1,0:T(8,128)(2,1)S(1)}, u32[]{:S(2)}, u32[]{:S(2)}) collective-permute-start(bf16[128,256]{1,0:T(8,128)(2,1)S(1)} %get-tuple-element.160), channel_id=1, source_target_pairs={{0,8},{8,16},{16,24},{24,32},{32,40},{40,48},{48,56},{56,64},{64,7... | collective-permute-start | bytes 196616 | tf_op jit(solution)/shard_map/while/body/eval_jaxpr/ppermute | solution.py:14
  33.1 5.6 %collective-permute-start.1 = (bf16[128,256]{1,0:T(8,128)(2,1)S(1)}, bf16[128,256]{1,0:T(8,128)(2,1)S(1)}, u32[]{:S(2)}, u32[]{:S(2)}) collective-permute-start(bf16[128,256]{1,0:T(8,128)(2,1)S(1)} %get-tuple-element.161), channel_id=1, source_target_pairs={{0,8},{8,16},{16,24},{24,32},{32,40},{40,48},{48,56},{56,64},{64,7... | collective-permute-start | bytes 196616 | tf_op jit(solution)/shard_map/while/body/eval_jaxpr/ppermute | solution.py:14
  35.1 5.6 %collective-permute-start = (bf16[128,256]{1,0:T(8,128)(2,1)S(1)}, bf16[128,256]{1,0:T(8,128)(2,1)S(1)}, u32[]{:S(2)}, u32[]{:S(2)}) collective-permute-start(bf16[128,256]{1,0:T(8,128)(2,1)S(1)} %get-tuple-element.160), channel_id=1, source_target_pairs={{0,8},{8,16},{16,24},{24,32},{32,40},{40,48},{48,56},{56,64},{64,7... | collective-permute-start | bytes 196616 | tf_op jit(solution)/shard_map/while/body/eval_jaxpr/ppermute | solution.py:14
  40.7 5.6 %collective-permute-start.1 = (bf16[128,256]{1,0:T(8,128)(2,1)S(1)}, bf16[128,256]{1,0:T(8,128)(2,1)S(1)}, u32[]{:S(2)}, u32[]{:S(2)}) collective-permute-start(bf16[128,256]{1,0:T(8,128)(2,1)S(1)} %get-tuple-element.161), channel_id=1, source_target_pairs={{0,8},{8,16},{16,24},{24,32},{32,40},{40,48},{48,56},{56,64},{64,7... | collective-permute-start | bytes 196616 | tf_op jit(solution)/shard_map/while/body/eval_jaxpr/ppermute | solution.py:14
  42.6 5.6 %collective-permute-start = (bf16[128,256]{1,0:T(8,128)(2,1)S(1)}, bf16[128,256]{1,0:T(8,128)(2,1)S(1)}, u32[]{:S(2)}, u32[]{:S(2)}) collective-permute-start(bf16[128,256]{1,0:T(8,128)(2,1)S(1)} %get-tuple-element.160), channel_id=1, source_target_pairs={{0,8},{8,16},{16,24},{24,32},{32,40},{40,48},{48,56},{56,64},{64,7... | collective-permute-start | bytes 196616 | tf_op jit(solution)/shard_map/while/body/eval_jaxpr/ppermute | solution.py:14
  48.3 5.6 %collective-permute-start.1 = (bf16[128,256]{1,0:T(8,128)(2,1)S(1)}, bf16[128,256]{1,0:T(8,128)(2,1)S(1)}, u32[]{:S(2)}, u32[]{:S(2)}) collective-permute-start(bf16[128,256]{1,0:T(8,128)(2,1)S(1)} %get-tuple-element.161), channel_id=1, source_target_pairs={{0,8},{8,16},{16,24},{24,32},{32,40},{40,48},{48,56},{56,64},{64,7... | collective-permute-start | bytes 196616 | tf_op jit(solution)/shard_map/while/body/eval_jaxpr/ppermute | solution.py:14
  50.2 5.6 %collective-permute-start = (bf16[128,256]{1,0:T(8,128)(2,1)S(1)}, bf16[128,256]{1,0:T(8,128)(2,1)S(1)}, u32[]{:S(2)}, u32[]{:S(2)}) collective-permute-start(bf16[128,256]{1,0:T(8,128)(2,1)S(1)} %get-tuple-element.160), channel_id=1, source_target_pairs={{0,8},{8,16},{16,24},{24,32},{32,40},{40,48},{48,56},{56,64},{64,7... | collective-permute-start | bytes 196616 | tf_op jit(solution)/shard_map/while/body/eval_jaxpr/ppermute | solution.py:14
  63.4 5.6 %collective-permute-start.1 = (bf16[128,256]{1,0:T(8,128)(2,1)S(1)}, bf16[128,256]{1,0:T(8,128)(2,1)S(1)}, u32[]{:S(2)}, u32[]{:S(2)}) collective-permute-start(bf16[128,256]{1,0:T(8,128)(2,1)S(1)} %get-tuple-element.161), channel_id=1, source_target_pairs={{0,8},{8,16},{16,24},{24,32},{32,40},{40,48},{48,56},{56,64},{64,7... | collective-permute-start | bytes 196616 | tf_op jit(solution)/shard_map/while/body/eval_jaxpr/ppermute | solution.py:14
  65.3 5.6 %collective-permute-start = (bf16[128,256]{1,0:T(8,128)(2,1)S(1)}, bf16[128,256]{1,0:T(8,128)(2,1)S(1)}, u32[]{:S(2)}, u32[]{:S(2)}) collective-permute-start(bf16[128,256]{1,0:T(8,128)(2,1)S(1)} %get-tuple-element.160), channel_id=1, source_target_pairs={{0,8},{8,16},{16,24},{24,32},{32,40},{40,48},{48,56},{56,64},{64,7... | collective-permute-start | bytes 196616 | tf_op jit(solution)/shard_map/while/body/eval_jaxpr/ppermute | solution.py:14
  71.0 5.6 %collective-permute-start.1 = (bf16[128,256]{1,0:T(8,128)(2,1)S(1)}, bf16[128,256]{1,0:T(8,128)(2,1)S(1)}, u32[]{:S(2)}, u32[]{:S(2)}) collective-permute-start(bf16[128,256]{1,0:T(8,128)(2,1)S(1)} %get-tuple-element.161), channel_id=1, source_target_pairs={{0,8},{8,16},{16,24},{24,32},{32,40},{40,48},{48,56},{56,64},{64,7... | collective-permute-start | bytes 196616 | tf_op jit(solution)/shard_map/while/body/eval_jaxpr/ppermute | solution.py:14
  72.9 5.6 %collective-permute-start = (bf16[128,256]{1,0:T(8,128)(2,1)S(1)}, bf16[128,256]{1,0:T(8,128)(2,1)S(1)}, u32[]{:S(2)}, u32[]{:S(2)}) collective-permute-start(bf16[128,256]{1,0:T(8,128)(2,1)S(1)} %get-tuple-element.160), channel_id=1, source_target_pairs={{0,8},{8,16},{16,24},{24,32},{32,40},{40,48},{48,56},{56,64},{64,7... | collective-permute-start | bytes 196616 | tf_op jit(solution)/shard_map/while/body/eval_jaxpr/ppermute | solution.py:14
  78.5 5.6 %collective-permute-start.1 = (bf16[128,256]{1,0:T(8,128)(2,1)S(1)}, bf16[128,256]{1,0:T(8,128)(2,1)S(1)}, u32[]{:S(2)}, u32[]{:S(2)}) collective-permute-start(bf16[128,256]{1,0:T(8,128)(2,1)S(1)} %get-tuple-element.161), channel_id=1, source_target_pairs={{0,8},{8,16},{16,24},{24,32},{32,40},{40,48},{48,56},{56,64},{64,7... | collective-permute-start | bytes 196616 | tf_op jit(solution)/shard_map/while/body/eval_jaxpr/ppermute | solution.py:14
  80.5 5.6 %collective-permute-start = (bf16[128,256]{1,0:T(8,128)(2,1)S(1)}, bf16[128,256]{1,0:T(8,128)(2,1)S(1)}, u32[]{:S(2)}, u32[]{:S(2)}) collective-permute-start(bf16[128,256]{1,0:T(8,128)(2,1)S(1)} %get-tuple-element.160), channel_id=1, source_target_pairs={{0,8},{8,16},{16,24},{24,32},{32,40},{40,48},{48,56},{56,64},{64,7... | collective-permute-start | bytes 196616 | tf_op jit(solution)/shard_map/while/body/eval_jaxpr/ppermute | solution.py:14
  86.1 6.2 %collective-permute-start.1 = (bf16[128,256]{1,0:T(8,128)(2,1)S(1)}, bf16[128,256]{1,0:T(8,128)(2,1)S(1)}, u32[]{:S(2)}, u32[]{:S(2)}) collective-permute-start(bf16[128,256]{1,0:T(8,128)(2,1)S(1)} %get-tuple-element.161), channel_id=1, source_target_pairs={{0,8},{8,16},{16,24},{24,32},{32,40},{40,48},{48,56},{56,64},{64,7... | collective-permute-start | bytes 196616 | tf_op jit(solution)/shard_map/while/body/eval_jaxpr/ppermute | solution.py:14
  88.0 5.6 %collective-permute-start = (bf16[128,256]{1,0:T(8,128)(2,1)S(1)}, bf16[128,256]{1,0:T(8,128)(2,1)S(1)}, u32[]{:S(2)}, u32[]{:S(2)}) collective-permute-start(bf16[128,256]{1,0:T(8,128)(2,1)S(1)} %get-tuple-element.160), channel_id=1, source_target_pairs={{0,8},{8,16},{16,24},{24,32},{32,40},{40,48},{48,56},{56,64},{64,7... | collective-permute-start | bytes 196616 | tf_op jit(solution)/shard_map/while/body/eval_jaxpr/ppermute | solution.py:14
  93.7 7.4 %collective-permute-start.1 = (bf16[128,256]{1,0:T(8,128)(2,1)S(1)}, bf16[128,256]{1,0:T(8,128)(2,1)S(1)}, u32[]{:S(2)}, u32[]{:S(2)}) collective-permute-start(bf16[128,256]{1,0:T(8,128)(2,1)S(1)} %get-tuple-element.161), channel_id=1, source_target_pairs={{0,8},{8,16},{16,24},{24,32},{32,40},{40,48},{48,56},{56,64},{64,7... | collective-permute-start | bytes 196616 | tf_op jit(solution)/shard_map/while/body/eval_jaxpr/ppermute | solution.py:14
  102.1 7.8 %collective-permute-start.1 = (bf16[128,256]{1,0:T(8,128)(2,1)S(1)}, bf16[128,256]{1,0:T(8,128)(2,1)S(1)}, u32[]{:S(2)}, u32[]{:S(2)}) collective-permute-start(bf16[128,256]{1,0:T(8,128)(2,1)S(1)} %get-tuple-element.161), channel_id=1, source_target_pairs={{0,8},{8,16},{16,24},{24,32},{32,40},{40,48},{48,56},{56,64},{64,7... | collective-permute-start | bytes 196616 | tf_op jit(solution)/shard_map/while/body/eval_jaxpr/ppermute | solution.py:14
  105.2 5.6 %collective-permute-start = (bf16[128,256]{1,0:T(8,128)(2,1)S(1)}, bf16[128,256]{1,0:T(8,128)(2,1)S(1)}, u32[]{:S(2)}, u32[]{:S(2)}) collective-permute-start(bf16[128,256]{1,0:T(8,128)(2,1)S(1)} %get-tuple-element.160), channel_id=1, source_target_pairs={{0,8},{8,16},{16,24},{24,32},{32,40},{40,48},{48,56},{56,64},{64,7... | collective-permute-start | bytes 196616 | tf_op jit(solution)/shard_map/while/body/eval_jaxpr/ppermute | solution.py:14
  110.8 7.8 %collective-permute-start.1 = (bf16[128,256]{1,0:T(8,128)(2,1)S(1)}, bf16[128,256]{1,0:T(8,128)(2,1)S(1)}, u32[]{:S(2)}, u32[]{:S(2)}) collective-permute-start(bf16[128,256]{1,0:T(8,128)(2,1)S(1)} %get-tuple-element.161), channel_id=1, source_target_pairs={{0,8},{8,16},{16,24},{24,32},{32,40},{40,48},{48,56},{56,64},{64,7... | collective-permute-start | bytes 196616 | tf_op jit(solution)/shard_map/while/body/eval_jaxpr/ppermute | solution.py:14
  119.6 7.8 %collective-permute-start.1 = (bf16[128,256]{1,0:T(8,128)(2,1)S(1)}, bf16[128,256]{1,0:T(8,128)(2,1)S(1)}, u32[]{:S(2)}, u32[]{:S(2)}) collective-permute-start(bf16[128,256]{1,0:T(8,128)(2,1)S(1)} %get-tuple-element.161), channel_id=1, source_target_pairs={{0,8},{8,16},{16,24},{24,32},{32,40},{40,48},{48,56},{56,64},{64,7... | collective-permute-start | bytes 196616 | tf_op jit(solution)/shard_map/while/body/eval_jaxpr/ppermute | solution.py:14
  128.4 7.8 %collective-permute-start.1 = (bf16[128,256]{1,0:T(8,128)(2,1)S(1)}, bf16[128,256]{1,0:T(8,128)(2,1)S(1)}, u32[]{:S(2)}, u32[]{:S(2)}) collective-permute-start(bf16[128,256]{1,0:T(8,128)(2,1)S(1)} %get-tuple-element.161), channel_id=1, source_target_pairs={{0,8},{8,16},{16,24},{24,32},{32,40},{40,48},{48,56},{56,64},{64,7... | collective-permute-start | bytes 196616 | tf_op jit(solution)/shard_map/while/body/eval_jaxpr/ppermute | solution.py:14
  (9 other events, 44.4 us)
Sparse Core Ops, SparseCore 0:
  147.2 95.1 reduce-scatter.1
where the time goes:
time: 254 us; the launch traced here: 251 us
  waiting for transfers between devices  137 us (54%)
  starting transfers between devices  83.8 us (33%)
  between operations  13.5 us (5%)
  local copies, waits for them, and re-layouts  5.82 us (2%)
  matrix products  5.77 us (2%)
  other arithmetic  4.7 us (2%)
    reduce_scatter x1, waiting for transfers between devices, per_device(): lax.psum_scatter(partial_out, 'head', scatter_dimension=1, tiled=True)  95.3 us
    ppermute x30, starting transfers between devices, shifted(): return lax.ppermute(value, axis, pairs)  83.8 us
    ppermute x30, waiting for transfers between devices, shifted(): return lax.ppermute(value, axis, pairs)  41.2 us
  transfers between devices with their start and end apart: 31, of which 24 were waited for; matrix products, arithmetic and copies ran while one was open for 0% of the time, Pallas kernels for 0%

commit v1 on v0

v1 whole, which is shorter than its diff:
```python
import jax
import jax.numpy as jnp
from jax import lax
from jax.sharding import PartitionSpec as P

HEADS = 32
KV_HEADS = 8
HEAD_DIM = 128


def chip_shift(value, chips, swap_core=False):
    devices = lax.axis_size("ctx")
    pairs = []
    for index in range(devices):
        target = (index + 2 * chips) % devices
        pairs.append((index, target ^ 1 if swap_core else target))
    return lax.ppermute(value, "ctx", pairs)


def per_device(queries, key_rows, values, doc_lengths, out_weight):
    my_index = lax.axis_index("ctx")
    head_index = lax.axis_index("head")
    head_devs = lax.axis_size("head")
    tok_rows = queries.shape[0]
    kv_width = key_rows.shape[1]
    local_heads = kv_width // HEAD_DIM
    group_size = HEADS // KV_HEADS
    score_scale = HEAD_DIM ** (-0.5)
    chip, core = my_index // 2, my_index % 2

    own = jnp.concatenate([key_rows, values], axis=1)
    back1 = chip_shift(own, 1)
    back7 = chip_shift(own, 7)
    back2 = chip_shift(back1, 1)
    back6 = chip_shift(back7, -1)
    back3 = chip_shift(back2, 1)
    back5 = chip_shift(back6, -1)
    back4 = chip_shift(back3, 1)
    back8 = chip_shift(own, 8, swap_core=True)
    local = jnp.concatenate([back7, back6, back5, back4, back3, back2, back1, own], axis=0)
    other = chip_shift(local, 0, swap_core=True)
    held = jnp.concatenate([back8, local, other], axis=0)

    rows = jnp.arange(tok_rows, dtype=jnp.int32)
    first = jnp.concatenate(
        [
            jnp.stack([(2 * (chip - 8) + 1 - core)]),
            2 * (chip - 7 + jnp.arange(8, dtype=jnp.int32)) + core,
            2 * (chip - 7 + jnp.arange(8, dtype=jnp.int32)) + 1 - core,
        ]
    )
    key_pos = (first[:, None] * tok_rows + rows[None, :]).reshape(-1)
    query_pos = my_index * tok_rows + rows
    doc_ends = jnp.cumsum(doc_lengths)
    doc_start = jnp.max(
        jnp.where(doc_ends[None, :] <= query_pos[:, None], doc_ends[None, :], 0), axis=1
    )
    allowed = (key_pos[None, :] >= doc_start[:, None]) & (key_pos[None, :] <= query_pos[:, None])
    pieces = []
    for pair in range(local_heads):
        query_block = queries[:, pair * group_size * HEAD_DIM : (pair + 1) * group_size * HEAD_DIM]
        query_block = query_block.reshape(tok_rows, group_size, HEAD_DIM)
        key_block = held[:, pair * HEAD_DIM : (pair + 1) * HEAD_DIM]
        value_block = held[:, kv_width + pair * HEAD_DIM : kv_width + (pair + 1) * HEAD_DIM]
        scores = (
            jnp.einsum("tgd,sd->gts", query_block, key_block, preferred_element_type=jnp.float32)
            * score_scale
        )
        scores = jnp.where(allowed[None], scores, -1e30)
        row_peak = jnp.max(scores, axis=2, keepdims=True)
        weights = jnp.exp(scores - row_peak)
        row_total = jnp.sum(weights, axis=2, keepdims=True)
        mixed_out = jnp.einsum(
            "gts,sd->gtd",
            weights.astype(jnp.bfloat16),
            value_block,
            preferred_element_type=jnp.float32,
        )
        mixed_out = mixed_out / row_total
        pieces.append(
            jnp.transpose(mixed_out, (1, 0, 2))
            .astype(jnp.bfloat16)
            .reshape(tok_rows, group_size * HEAD_DIM)
        )
    attended = jnp.concatenate(pieces, axis=1)
    width = out_weight.shape[1] // head_devs
    partial_out = jnp.dot(attended, out_weight, preferred_element_type=jnp.float32)

    def part(ahead):
        return lax.dynamic_slice_in_dim(
            partial_out, lax.rem(head_index + ahead, head_devs) * width, width, 1
        )

    total = part(0)
    for ahead in (2, 1, 3):
        got = lax.ppermute(
            part(ahead).astype(jnp.bfloat16),
            "head",
            [(i, (i + ahead) % head_devs) for i in range(head_devs)],
        )
        total = total + got.astype(jnp.float32)
    return total.astype(jnp.bfloat16)


def solution(mesh):
    return jax.shard_map(
        per_device,
        mesh=mesh,
        in_specs=(
            P(("batch", "ctx"), "head"),
            P(("batch", "ctx"), "head"),
            P(("batch", "ctx"), "head"),
            P("batch"),
            P("head", None),
        ),
        out_specs=P(("batch", "ctx"), "head"),
        check_vma=False,
    )
```

time: 254 us -> 114 us (0.45)
  the two profiles are of different devices: /device:TPU:16 before, /device:TPU:3 now
where the time goes in v1:
time: 114 us; the launch traced here: 113 us
  starting transfers between devices  53.1 us (47%)
  waiting for transfers between devices  42.8 us (38%)
  local copies, waits for them, and re-layouts  6.95 us (6%)
  matrix products  5.39 us (5%)
  other arithmetic  4.48 us (4%)
    ppermute x9, starting transfers between devices, chip_shift(): return lax.ppermute(value, 'ctx', pairs)  39.5 us
    ppermute x3, waiting for transfers between devices, per_device(): lax.ppermute(part(ahead).astype(jnp.bfloat16), 'head', [(i, (i + ahead) %...  21.7 us
    ppermute x9, waiting for transfers between devices, chip_shift(): return lax.ppermute(value, 'ctx', pairs)  21.2 us
    ppermute x3, starting transfers between devices, per_device(): lax.ppermute(part(ahead).astype(jnp.bfloat16), 'head', [(i, (i + ahead) %...  13.6 us
    unnamed x26, local copies, waits for them, and re-layouts  3.85 us
    dot_general x2, matrix products, per_device(): jnp.einsum('tgd,sd->gts', query_block, key_block, preferred_element_type=...  2.53 us
  transfers between devices with their start and end apart: 12, of which 7 were waited for; matrix products, arithmetic and copies ran while one was open for 3% of the time, Pallas kernels for 0%

profile of v1, /device:TPU:3, one launch (start us, length us, event | category | flops | bytes accessed | tf_op | source)
XLA Modules:
  0.0 113.2 jit_solution(12400742561628379575)
XLA Ops:
  1.8 5.9 %collective-permute-start.1 = (bf16[128,512]{1,0:T(8,128)(2,1)S(1)}, bf16[128,512]{1,0:T(8,128)(2,1)S(1)}, u32[]{:S(2)}, u32[]{:S(2)}) collective-permute-start(bf16[128,512]{1,0:T(8,128)(2,1)S(1)} %constant_dynamic-update-slice_fusion), channel_id=1, source_target_pairs={{0,112},{8,120},{16,128},{24,136},{32,144},{40,152},{48,160},{56,1... | collective-permute-start | bytes 393224 | tf_op jit(solution)/shard_map/ppermute | solution.py:17
  7.7 5.8 %collective-permute-start = (bf16[128,512]{1,0:T(8,128)(2,1)S(1)}, bf16[128,512]{1,0:T(8,128)(2,1)S(1)}, u32[]{:S(2)}, u32[]{:S(2)}) collective-permute-start(bf16[128,512]{1,0:T(8,128)(2,1)S(1)} %constant_dynamic-update-slice_fusion), channel_id=1, source_target_pairs={{0,136},{8,128},{16,152},{24,144},{32,168},{40,160},{48,184},{56,1... | collective-permute-start | bytes 393224 | tf_op jit(solution)/shard_map/ppermute | solution.py:17
  13.4 2.1 %collective-permute-start.4 = (bf16[128,512]{1,0:T(8,128)(2,1)S(1)}, bf16[128,512]{1,0:T(8,128)(2,1)S(1)}, u32[]{:S(2)}, u32[]{:S(2)}) collective-permute-start(bf16[128,512]{1,0:T(8,128)(2,1)S(1)} %constant_dynamic-update-slice_fusion), channel_id=1, source_target_pairs={{0,16},{8,24},{16,32},{24,40},{32,48},{40,56},{48,64},{56,72},{64,... | collective-permute-start | bytes 393224 | tf_op jit(solution)/shard_map/ppermute | solution.py:17
  15.5 1.0 fusion.38
  16.5 13.0 %collective-permute-done.4 = bf16[128,512]{1,0:T(8,128)(2,1)S(1)} collective-permute-done((bf16[128,512]{1,0:T(8,128)(2,1)S(1)}, bf16[128,512]{1,0:T(8,128)(2,1)S(1)}, u32[]{:S(2)}, u32[]{:S(2)}) %collective-permute-start.4) | collective-permute-done | bytes 131104 | tf_op jit(solution)/shard_map/ppermute | solution.py:17
  29.5 1.9 %collective-permute-start.5 = (bf16[128,512]{1,0:T(8,128)(2,1)S(1)}, bf16[128,512]{1,0:T(8,128)(2,1)S(1)}, u32[]{:S(2)}, u32[]{:S(2)}) collective-permute-start(bf16[128,512]{1,0:T(8,128)(2,1)S(1)} %collective-permute-done.4), channel_id=1, source_target_pairs={{0,16},{8,24},{16,32},{24,40},{32,48},{40,56},{48,64},{56,72},{64,... | collective-permute-start | bytes 393224 | tf_op jit(solution)/shard_map/ppermute | solution.py:17
  31.5 6.7 %collective-permute-start.2 = (bf16[128,512]{1,0:T(8,128)(2,1)S(1)}, bf16[128,512]{1,0:T(8,128)(2,1)S(1)}, u32[]{:S(2)}, u32[]{:S(2)}) collective-permute-start(bf16[128,512]{1,0:T(8,128)(2,1)S(1)} %collective-permute-done.1), channel_id=1, source_target_pairs={{0,1008},{8,1016},{16,0},{24,8},{32,16},{40,24},{48,32},{56,40},{6... | collective-permute-start | bytes 393224 | tf_op jit(solution)/shard_map/ppermute | solution.py:17
  38.6 1.9 %collective-permute-start.6 = (bf16[128,512]{1,0:T(8,128)(2,1)S(1)}, bf16[128,512]{1,0:T(8,128)(2,1)S(1)}, u32[]{:S(2)}, u32[]{:S(2)}) collective-permute-start(bf16[128,512]{1,0:T(8,128)(2,1)S(1)} %collective-permute-done.5), channel_id=1, source_target_pairs={{0,16},{8,24},{16,32},{24,40},{32,48},{40,56},{48,64},{56,72},{64,... | collective-permute-start | bytes 393224 | tf_op jit(solution)/shard_map/ppermute | solution.py:17
  40.5 6.7 %collective-permute-start.3 = (bf16[128,512]{1,0:T(8,128)(2,1)S(1)}, bf16[128,512]{1,0:T(8,128)(2,1)S(1)}, u32[]{:S(2)}, u32[]{:S(2)}) collective-permute-start(bf16[128,512]{1,0:T(8,128)(2,1)S(1)} %collective-permute-done.2), channel_id=1, source_target_pairs={{0,1008},{8,1016},{16,0},{24,8},{32,16},{40,24},{48,32},{56,40},{6... | collective-permute-start | bytes 393224 | tf_op jit(solution)/shard_map/ppermute | solution.py:17
  47.6 1.9 %collective-permute-start.7 = (bf16[128,512]{1,0:T(8,128)(2,1)S(1)}, bf16[128,512]{1,0:T(8,128)(2,1)S(1)}, u32[]{:S(2)}, u32[]{:S(2)}) collective-permute-start(bf16[128,512]{1,0:T(8,128)(2,1)S(1)} %collective-permute-done.6), channel_id=1, source_target_pairs={{0,16},{8,24},{16,32},{24,40},{32,48},{40,56},{48,64},{56,72},{64,... | collective-permute-start | bytes 393224 | tf_op jit(solution)/shard_map/ppermute | solution.py:17
  49.6 7.0 %collective-permute-done.7 = bf16[128,512]{1,0:T(8,128)(2,1)S(1)} collective-permute-done((bf16[128,512]{1,0:T(8,128)(2,1)S(1)}, bf16[128,512]{1,0:T(8,128)(2,1)S(1)}, u32[]{:S(2)}, u32[]{:S(2)}) %collective-permute-start.7) | collective-permute-done | bytes 131104 | tf_op jit(solution)/shard_map/ppermute | solution.py:17
  56.8 6.7 %collective-permute-start.8 = (bf16[1024,512]{1,0:T(8,128)(2,1)S(1)}, bf16[1024,512]{1,0:T(8,128)(2,1)S(1)}, u32[]{:S(2)}, u32[]{:S(2)}) collective-permute-start(bf16[1024,512]{1,0:T(8,128)(2,1)S(1)} %get-tuple-element.24), channel_id=1, source_target_pairs={{0,8},{8,0},{16,24},{24,16},{32,40},{40,32},{48,56},{56,48},{64,72... | collective-permute-start | bytes 3145736 | tf_op jit(solution)/shard_map/ppermute | solution.py:17
  64.3 1.0 compare_and_fusion
  65.8 1.0 constant_dynamic-update-slice_fusion.10
  66.8 1.8 %fusion.40 = (f32[4,128]{1,0:T(4,128)S(1)}, f32[4,128,2176]{1,2,0:T(8,128)S(1)}) fusion(bf16[128,4,128]{0,2,1:T(8,128)(2,1)S(1)} %bitcast.54, bf16[2176,512]{1,0:T(8,128)(2,1)} %constant_dynamic-update-slice_fusion.10, pred[128,2176]{0,1:T(8,128)(4,1)S(1)} %compare_and_fusion), kind=kOutput, calls=%fused_computation.67 | convolution fusion | flops 288554496 | bytes 5425152 | tf_op jit(solution)/shard_map/tgd,sd->gts/dot_general | solution.py:66
  69.2 1.0 copy-done.3
  73.2 1.5 %slice-done.1 = s8[4194304]{0:T(1024)(128)(4,1)S(1)} async-done(((s8[8388608]{0:T(1024)(128)(4,1)}), s8[4194304]{0:T(1024)(128)(4,1)S(1)}, s32[]{:S(2)}) %slice-start.1) | async-done | bytes 4194328
  74.7 1.3 %fusion.32 = f32[128,4096]{1,0:T(8,128)S(1)} fusion(bf16[1024,4096]{1,0:T(8,128)(2,1)S(1)} %bitcast.50, bf16[128,512]{0,1:T(8,128)(2,1)S(1)} %bitcast.52, bf16[128,512]{0,1:T(8,128)(2,1)S(1)} %bitcast.51), kind=kOutput, calls=%fused_computation.31 | convolution fusion | flops 1074266112 | bytes 10747904 | tf_op jit(solution)/shard_map/dot_general | solution.py:87
  76.1 4.0 %collective-permute-start.10 = (bf16[128,1024]{1,0:T(8,128)(2,1)S(1)}, bf16[128,1024]{1,0:T(8,128)(2,1)S(1)}, u32[]{:S(2)}, u32[]{:S(2)}) collective-permute-start(bf16[128,1024]{1,0:T(8,128)(2,1)S(1)} %get-tuple-element.7), channel_id=1, source_target_pairs={{0,2},{2,4},{4,6},{6,0},{1,3},{3,5},{5,7},{7,1},{8,10},{10,12},{12... | collective-permute-start | bytes 786440 | tf_op jit(solution)/shard_map/ppermute | solution.py:96
  80.2 3.3 %collective-permute-start.11 = (bf16[128,1024]{1,0:T(8,128)(2,1)S(1)}, bf16[128,1024]{1,0:T(8,128)(2,1)S(1)}, u32[]{:S(2)}, u32[]{:S(2)}) collective-permute-start(bf16[128,1024]{1,0:T(8,128)(2,1)S(1)} %get-tuple-element.6), channel_id=1, source_target_pairs={{0,6},{2,0},{4,2},{6,4},{1,7},{3,1},{5,3},{7,5},{8,14},{10,8},{12,... | collective-permute-start | bytes 786440 | tf_op jit(solution)/shard_map/ppermute | solution.py:96
  83.5 6.2 %collective-permute-start.9 = (bf16[128,1024]{1,0:T(8,128)(2,1)S(1)}, bf16[128,1024]{1,0:T(8,128)(2,1)}, u32[]{:S(2)}, u32[]{:S(2)}) collective-permute-start(bf16[128,1024]{1,0:T(8,128)(2,1)S(1)} %get-tuple-element.5), channel_id=1, source_target_pairs={{0,4},{2,6},{4,0},{6,2},{1,5},{3,7},{5,1},{7,3},{8,12},{10,14},{12... | collective-permute-start | bytes 786440 | tf_op jit(solution)/shard_map/ppermute | solution.py:96
  89.7 5.6 %collective-permute-done.10 = bf16[128,1024]{1,0:T(8,128)(2,1)S(1)} collective-permute-done((bf16[128,1024]{1,0:T(8,128)(2,1)S(1)}, bf16[128,1024]{1,0:T(8,128)(2,1)S(1)}, u32[]{:S(2)}, u32[]{:S(2)}) %collective-permute-start.10) | collective-permute-done | bytes 262176 | tf_op jit(solution)/shard_map/ppermute | solution.py:96
  95.4 16.0 %collective-permute-done.9 = bf16[128,1024]{1,0:T(8,128)(2,1)} collective-permute-done((bf16[128,1024]{1,0:T(8,128)(2,1)S(1)}, bf16[128,1024]{1,0:T(8,128)(2,1)}, u32[]{:S(2)}, u32[]{:S(2)}) %collective-permute-start.9) | collective-permute-done | bytes 262176 | tf_op jit(solution)/shard_map/ppermute | solution.py:96
  111.4 1.8 %add_convert_fusion = bf16[128,1024]{1,0:T(8,128)(2,1)} fusion(bf16[128,1024]{1,0:T(8,128)(2,1)S(1)} %collective-permute-done.11, bf16[128,1024]{1,0:T(8,128)(2,1)S(1)} %collective-permute-done.10, bf16[128,1024]{1,0:T(8,128)(2,1)} %collective-permute-done.9, f32[128,4096]{1,0:T(8,128)S(1)} %fusion.32, s32[]{:T(128)S(6)} %select_n.39), kind=kLoop, calls=%fused_computation.27 | loop fusion | flops 917504 | bytes 1572868 | tf_op jit(solution)/shard_map/convert_element_type | solution.py:102
  (49 shorter events, 7.6 us)
Async XLA Ops:
  0.0 56.7 %copy-start = (bf16[128,256]{1,0:T(8,128)(2,1)S(1)}, bf16[128,256]{1,0:T(8,128)(2,1)}, u32[]{:S(2)}) copy-start(bf16[128,256]{1,0:T(8,128)(2,1)} %param.6) | copy-start | bytes 196612
  0.0 56.7 %copy-start.1 = (bf16[128,256]{1,0:T(8,128)(2,1)S(1)}, bf16[128,256]{1,0:T(8,128)(2,1)}, u32[]{:S(2)}) copy-start(bf16[128,256]{1,0:T(8,128)(2,1)} %param.7) | copy-start | bytes 196612
  0.0 63.6 %copy-start.4 = (s32[64]{0:T(128)S(1)}, s32[64]{0:T(128)}, u32[]{:S(2)}) copy-start(s32[64]{0:T(128)} %param.8) | copy-start | bytes 772
  1.8 29.7 %collective-permute-start.1 = (bf16[128,512]{1,0:T(8,128)(2,1)S(1)}, bf16[128,512]{1,0:T(8,128)(2,1)S(1)}, u32[]{:S(2)}, u32[]{:S(2)}) collective-permute-start(bf16[128,512]{1,0:T(8,128)(2,1)S(1)} %constant_dynamic-update-slice_fusion), channel_id=1, source_target_pairs={{0,112},{8,120},{16,128},{24,136},{32,144},{40,152},{48,160},{56,1... | collective-permute-start | bytes 393224 | tf_op jit(solution)/shard_map/ppermute | solution.py:17
  7.7 32.8 %collective-permute-start = (bf16[128,512]{1,0:T(8,128)(2,1)S(1)}, bf16[128,512]{1,0:T(8,128)(2,1)S(1)}, u32[]{:S(2)}, u32[]{:S(2)}) collective-permute-start(bf16[128,512]{1,0:T(8,128)(2,1)S(1)} %constant_dynamic-update-slice_fusion), channel_id=1, source_target_pairs={{0,136},{8,128},{16,152},{24,144},{32,168},{40,160},{48,184},{56,1... | collective-permute-start | bytes 393224 | tf_op jit(solution)/shard_map/ppermute | solution.py:17
  13.4 16.1 %collective-permute-start.4 = (bf16[128,512]{1,0:T(8,128)(2,1)S(1)}, bf16[128,512]{1,0:T(8,128)(2,1)S(1)}, u32[]{:S(2)}, u32[]{:S(2)}) collective-permute-start(bf16[128,512]{1,0:T(8,128)(2,1)S(1)} %constant_dynamic-update-slice_fusion), channel_id=1, source_target_pairs={{0,16},{8,24},{16,32},{24,40},{32,48},{40,56},{48,64},{56,72},{64,... | collective-permute-start | bytes 393224 | tf_op jit(solution)/shard_map/ppermute | solution.py:17
  29.5 9.0 %collective-permute-start.5 = (bf16[128,512]{1,0:T(8,128)(2,1)S(1)}, bf16[128,512]{1,0:T(8,128)(2,1)S(1)}, u32[]{:S(2)}, u32[]{:S(2)}) collective-permute-start(bf16[128,512]{1,0:T(8,128)(2,1)S(1)} %collective-permute-done.4), channel_id=1, source_target_pairs={{0,16},{8,24},{16,32},{24,40},{32,48},{40,56},{48,64},{56,72},{64,... | collective-permute-start | bytes 393224 | tf_op jit(solution)/shard_map/ppermute | solution.py:17
  31.5 9.0 %collective-permute-start.2 = (bf16[128,512]{1,0:T(8,128)(2,1)S(1)}, bf16[128,512]{1,0:T(8,128)(2,1)S(1)}, u32[]{:S(2)}, u32[]{:S(2)}) collective-permute-start(bf16[128,512]{1,0:T(8,128)(2,1)S(1)} %collective-permute-done.1), channel_id=1, source_target_pairs={{0,1008},{8,1016},{16,0},{24,8},{32,16},{40,24},{48,32},{56,40},{6... | collective-permute-start | bytes 393224 | tf_op jit(solution)/shard_map/ppermute | solution.py:17
  38.6 9.0 %collective-permute-start.6 = (bf16[128,512]{1,0:T(8,128)(2,1)S(1)}, bf16[128,512]{1,0:T(8,128)(2,1)S(1)}, u32[]{:S(2)}, u32[]{:S(2)}) collective-permute-start(bf16[128,512]{1,0:T(8,128)(2,1)S(1)} %collective-permute-done.5), channel_id=1, source_target_pairs={{0,16},{8,24},{16,32},{24,40},{32,48},{40,56},{48,64},{56,72},{64,... | collective-permute-start | bytes 393224 | tf_op jit(solution)/shard_map/ppermute | solution.py:17
  40.5 9.0 %collective-permute-start.3 = (bf16[128,512]{1,0:T(8,128)(2,1)S(1)}, bf16[128,512]{1,0:T(8,128)(2,1)S(1)}, u32[]{:S(2)}, u32[]{:S(2)}) collective-permute-start(bf16[128,512]{1,0:T(8,128)(2,1)S(1)} %collective-permute-done.2), channel_id=1, source_target_pairs={{0,1008},{8,1016},{16,0},{24,8},{32,16},{40,24},{48,32},{56,40},{6... | collective-permute-start | bytes 393224 | tf_op jit(solution)/shard_map/ppermute | solution.py:17
  47.6 9.0 %collective-permute-start.7 = (bf16[128,512]{1,0:T(8,128)(2,1)S(1)}, bf16[128,512]{1,0:T(8,128)(2,1)S(1)}, u32[]{:S(2)}, u32[]{:S(2)}) collective-permute-start(bf16[128,512]{1,0:T(8,128)(2,1)S(1)} %collective-permute-done.6), channel_id=1, source_target_pairs={{0,16},{8,24},{16,32},{24,40},{32,48},{40,56},{48,64},{56,72},{64,... | collective-permute-start | bytes 393224 | tf_op jit(solution)/shard_map/ppermute | solution.py:17
  56.8 6.7 %copy-start.2 = (bf16[2176,512]{1,0:T(8,128)(2,1)}, bf16[2176,512]{1,0:T(8,128)(2,1)S(1)}, u32[]{:S(2)}) copy-start(bf16[2176,512]{1,0:T(8,128)(2,1)S(1)} %get-tuple-element.25) | copy-start | bytes 6684676
  56.8 9.0 %collective-permute-start.8 = (bf16[1024,512]{1,0:T(8,128)(2,1)S(1)}, bf16[1024,512]{1,0:T(8,128)(2,1)S(1)}, u32[]{:S(2)}, u32[]{:S(2)}) collective-permute-start(bf16[1024,512]{1,0:T(8,128)(2,1)S(1)} %get-tuple-element.24), channel_id=1, source_target_pairs={{0,8},{8,0},{16,24},{24,16},{32,40},{40,32},{48,56},{56,48},{64,72... | collective-permute-start | bytes 3145736 | tf_op jit(solution)/shard_map/ppermute | solution.py:17
  68.6 1.6 %copy-start.3 = (bf16[2176,512]{1,0:T(8,128)(2,1)S(1)}, bf16[2176,512]{1,0:T(8,128)(2,1)}, u32[]{:S(2)}) copy-start(bf16[2176,512]{1,0:T(8,128)(2,1)} %constant_dynamic-update-slice_fusion.10) | copy-start | bytes 6684676
  71.0 2.2 %slice-start = ((s8[8388608]{0:T(1024)(128)(4,1)}), s8[4194304]{0:T(1024)(128)(4,1)S(1)}, s32[]{:S(2)}) async-start(s8[8388608]{0:T(1024)(128)(4,1)} %bitcast.49), calls=%async_computation | async-start | bytes 8388608
  71.8 2.9 %slice-start.1 = ((s8[8388608]{0:T(1024)(128)(4,1)}), s8[4194304]{0:T(1024)(128)(4,1)S(1)}, s32[]{:S(2)}) async-start(s8[8388608]{0:T(1024)(128)(4,1)} %bitcast.49), calls=%async_computation.1 | async-start | bytes 8388608
  76.1 19.3 %collective-permute-start.10 = (bf16[128,1024]{1,0:T(8,128)(2,1)S(1)}, bf16[128,1024]{1,0:T(8,128)(2,1)S(1)}, u32[]{:S(2)}, u32[]{:S(2)}) collective-permute-start(bf16[128,1024]{1,0:T(8,128)(2,1)S(1)} %get-tuple-element.7), channel_id=1, source_target_pairs={{0,2},{2,4},{4,6},{6,0},{1,3},{3,5},{5,7},{7,1},{8,10},{10,12},{12... | collective-permute-start | bytes 786440 | tf_op jit(solution)/shard_map/ppermute | solution.py:96
  80.2 15.2 %collective-permute-start.11 = (bf16[128,1024]{1,0:T(8,128)(2,1)S(1)}, bf16[128,1024]{1,0:T(8,128)(2,1)S(1)}, u32[]{:S(2)}, u32[]{:S(2)}) collective-permute-start(bf16[128,1024]{1,0:T(8,128)(2,1)S(1)} %get-tuple-element.6), channel_id=1, source_target_pairs={{0,6},{2,0},{4,2},{6,4},{1,7},{3,1},{5,3},{7,5},{8,14},{10,8},{12,... | collective-permute-start | bytes 786440 | tf_op jit(solution)/shard_map/ppermute | solution.py:96
  83.5 27.9 %collective-permute-start.9 = (bf16[128,1024]{1,0:T(8,128)(2,1)S(1)}, bf16[128,1024]{1,0:T(8,128)(2,1)}, u32[]{:S(2)}, u32[]{:S(2)}) collective-permute-start(bf16[128,1024]{1,0:T(8,128)(2,1)S(1)} %get-tuple-element.5), channel_id=1, source_target_pairs={{0,4},{2,6},{4,0},{6,2},{1,5},{3,7},{5,1},{7,3},{8,12},{10,14},{12... | collective-permute-start | bytes 786440 | tf_op jit(solution)/shard_map/ppermute | solution.py:96

commit v2 on v0

v2 whole, which is shorter than its diff:
```python
import math

import jax
import jax.numpy as jnp
from jax import lax
from jax.experimental import pallas as pl
from jax.experimental.pallas import tpu as pltpu
from jax.sharding import PartitionSpec as P


HEADS = 32
KV_HEADS = 8
HEAD_DIM = 128
GROUP = HEADS // KV_HEADS
ROWS = 128
FAR = 1e30
BACK = 7
EXP_SCALE = HEAD_DIM ** (-0.5) * math.log2(math.e)


def chip_send(value, chips, targets):
    pairs = []
    for target in targets:
        if 0 <= target - chips < lax.axis_size("ctx") // 2:
            pairs += [(2 * (target - chips) + core, 2 * target + core) for core in range(2)]
    return lax.ppermute(value, "ctx", pairs)


def gather_blocks(own):
    chips = lax.axis_size("ctx") // 2
    back = {}
    back[1] = chip_send(own, 1, range(1, chips))
    back[7] = chip_send(own, 7, range(7, chips))
    for step in range(2, 5):
        back[step] = chip_send(back[step - 1], 1, range(step, chips))
        far = 8 - step
        if far > 4:
            relayed = chip_send(back[far + 1], -1, range(far, chips - step + 1))
            direct = chip_send(own, far, range(chips - step + 1, chips))
            back[far] = relayed + direct
    return back


def head_swap(value, stage):
    heads = lax.axis_size("head")
    pairs = []
    for index in range(lax.axis_size("ctx")):
        for head in range(heads):
            partner = head ^ 1 if (stage + index) % 2 == 0 else heads - 1 - head
            pairs.append((index * heads + head, index * heads + partner))
    return lax.ppermute(value, ("ctx", "head"), pairs)


def masked_bias(first, start_ref, query_first):
    lane = lax.broadcasted_iota(jnp.int32, (ROWS, ROWS), 1)
    row = lax.broadcasted_iota(jnp.int32, (ROWS, ROWS), 0)
    key_pos = lane + first
    keep = (key_pos >= start_ref[...]) & (key_pos <= row + query_first)
    return jnp.where(keep, 0.0, -FAR).astype(jnp.float32)


def stacked_queries(q_ref, pair):
    return jnp.concatenate(
        [
            q_ref[:, (pair * GROUP + h) * HEAD_DIM : (pair * GROUP + h + 1) * HEAD_DIM]
            for h in range(GROUP)
        ],
        axis=0,
    )


def biased_scores(q_ref, keys, bias, pair):
    scores = lax.dot_general(
        stacked_queries(q_ref, pair),
        keys,
        (((1,), (1,)), ((), ())),
        preferred_element_type=jnp.float32,
    )
    count = keys.shape[0]
    return (scores.reshape(GROUP, ROWS, count) + bias[None]).reshape(GROUP * ROWS, count)


def document_starts(length_ref, query_first):
    query_pos = lax.broadcasted_iota(jnp.int32, (8, ROWS), 1) + query_first
    starts = jnp.zeros_like(query_pos)
    end = jnp.int32(0)
    for i in range(length_ref.shape[0]):
        end = end + length_ref[i]
        starts = jnp.where(query_pos >= end, end, starts)
    return jnp.broadcast_to(starts[:1], (ROWS, ROWS)).T


def local_kernel(first_ref, length_ref, q_hbm, w_hbm, *refs):
    blocks, (peak_ref, total_ref, mixed_ref, start_ref, q_ref, w_ref, sems) = refs[:-7], refs[-7:]
    fetch_q = pltpu.make_async_copy(q_hbm, q_ref, sems.at[0])
    fetch_w = pltpu.make_async_copy(w_hbm.at[: w_ref.shape[0]], w_ref, sems.at[1])
    fetch_q.start()
    fetch_w.start()
    start_ref[...] = document_starts(length_ref, first_ref[len(blocks)])
    kv_width = blocks[0].shape[1] // 2
    bias = jnp.concatenate(
        [masked_bias(first_ref[i], start_ref, first_ref[len(blocks)]) for i in range(len(blocks))],
        axis=1,
    )
    fetch_q.wait()
    for pair in range(kv_width // HEAD_DIM):
        low, high = pair * HEAD_DIM, (pair + 1) * HEAD_DIM
        keys = jnp.concatenate([b[:, low:high] for b in blocks], axis=0)
        vals = jnp.concatenate([b[:, kv_width + low : kv_width + high] for b in blocks], axis=0)
        scores = biased_scores(q_ref, keys, bias, pair)
        peak = jnp.max(scores, axis=1, keepdims=True)
        weights = jnp.exp2((scores - peak) * EXP_SCALE)
        rows = slice(pair * GROUP * ROWS, (pair + 1) * GROUP * ROWS)
        wide = (GROUP * ROWS, HEAD_DIM)
        peak_ref[rows, :] = jnp.broadcast_to(peak, wide)
        total_ref[rows, :] = jnp.broadcast_to(jnp.sum(weights, axis=1, keepdims=True), wide)
        mixed_ref[rows, :] = jnp.dot(
            weights.astype(jnp.bfloat16), vals, preferred_element_type=jnp.float32
        )
    fetch_w.wait()


def project(attended, weights, column):
    rows, width = weights[0].shape[0], ROWS * GROUP * 2
    at = pl.multiple_of(column * width, width)
    return sum(
        jnp.dot(
            attended[:, i * rows : (i + 1) * rows],
            half[:, pl.ds(at, width)],
            preferred_element_type=jnp.float32,
        )
        for i, half in enumerate(weights)
    )


def rest_kernel(
    first_ref,
    w_hbm,
    other_ref,
    peak_ref,
    total_ref,
    mixed_ref,
    start_ref,
    q_ref,
    w_ref,
    *refs,
):
    outs, (attended_ref, w_rest_ref, sem) = refs[:-3], refs[-3:]
    fetch_w = pltpu.make_async_copy(w_hbm.at[w_ref.shape[0] :], w_rest_ref, sem)
    fetch_w.start()
    kv_width = other_ref.shape[1] // 2
    blocks = other_ref.shape[0] // ROWS
    bias = jnp.concatenate(
        [masked_bias(first_ref[i], start_ref, first_ref[blocks]) for i in range(blocks)], axis=1
    )
    for pair in range(kv_width // HEAD_DIM):
        low, high = pair * HEAD_DIM, (pair + 1) * HEAD_DIM
        scores = biased_scores(q_ref, other_ref[:, low:high], bias, pair)
        rows = slice(pair * GROUP * ROWS, (pair + 1) * GROUP * ROWS)
        old_peak = peak_ref[rows, :]
        peak = jnp.maximum(old_peak, jnp.max(scores, axis=1, keepdims=True))
        weights = jnp.exp2((scores - peak[:, :1]) * EXP_SCALE)
        keep = jnp.exp2((old_peak - peak) * EXP_SCALE)
        total = total_ref[rows, :] * keep + jnp.sum(weights, axis=1, keepdims=True)
        mixed = mixed_ref[rows, :] * keep + jnp.dot(
            weights.astype(jnp.bfloat16),
            other_ref[:, kv_width + low : kv_width + high],
            preferred_element_type=jnp.float32,
        )
        mixed = (mixed / total).astype(jnp.bfloat16)
        for h in range(GROUP):
            at = (pair * GROUP + h) * HEAD_DIM
            attended_ref[:, at : at + HEAD_DIM] = mixed[h * ROWS : (h + 1) * ROWS]
    fetch_w.wait()
    for i, out in enumerate(outs):
        part = project(attended_ref[...], (w_ref, w_rest_ref), first_ref[blocks + 1 + i])
        out[...] = part.astype(out.dtype)


def vmem(count):
    return [pl.BlockSpec(memory_space=pltpu.VMEM)] * count


def join_kernel(*refs):
    blocks, (first_ref, out_ref, first_out) = refs[:-3], refs[-3:]
    for i, block in enumerate(blocks):
        out_ref[i * ROWS : (i + 1) * ROWS, :] = block[...]
    first_out[...] = first_ref[...]


def join(blocks, cross):
    shape = (len(blocks) * ROWS, blocks[0].shape[1])
    return pl.pallas_call(
        join_kernel,
        out_shape=(
            jax.ShapeDtypeStruct(shape, blocks[0].dtype),
            jax.ShapeDtypeStruct(cross.shape, cross.dtype),
        ),
        in_specs=vmem(len(blocks) + 1),
        out_specs=tuple(vmem(2)),
        compiler_params=pltpu.CompilerParams(vmem_limit_bytes=4 * 2**20),
        name="join",
    )(*blocks, cross)


def half_weight(out_weight):
    rows, columns = out_weight.shape
    return jax.ShapeDtypeStruct((rows // 2, columns), out_weight.dtype)


def attend_local(firsts, doc_lengths, queries, out_weight, blocks):
    rows = queries.shape[0] * queries.shape[1] // HEAD_DIM
    state = jax.ShapeDtypeStruct((rows, HEAD_DIM), jnp.float32)
    keys = ROWS * len(blocks)
    return pl.pallas_call(
        local_kernel,
        out_shape=(state,) * 3
        + (
            jax.ShapeDtypeStruct((ROWS, ROWS), jnp.int32),
            jax.ShapeDtypeStruct(queries.shape, queries.dtype),
            half_weight(out_weight),
        ),
        in_specs=[pl.BlockSpec(memory_space=pltpu.SMEM)] * 2
        + [pl.BlockSpec(memory_space=pltpu.HBM)] * 2
        + vmem(len(blocks)),
        out_specs=tuple(vmem(6)),
        scratch_shapes=[pltpu.SemaphoreType.DMA((2,))],
        compiler_params=pltpu.CompilerParams(vmem_limit_bytes=16 * 2**20),
        cost_estimate=pl.CostEstimate(
            flops=4 * rows * keys * HEAD_DIM,
            bytes_accessed=4 * rows * keys,
            transcendentals=rows * keys,
        ),
        name="attend_local",
    )(firsts, doc_lengths, queries, out_weight, *blocks)


def attend_rest(firsts, out_weight, other, state, width):
    queries = state[-2]
    rows = queries.shape[0] * queries.shape[1] // HEAD_DIM
    keys = other.shape[0]
    half = half_weight(out_weight)
    kinds = (jnp.bfloat16, jnp.bfloat16, jnp.float32, jnp.float32)
    return pl.pallas_call(
        rest_kernel,
        out_shape=tuple(jax.ShapeDtypeStruct((queries.shape[0], width), k) for k in kinds),
        in_specs=[
            pl.BlockSpec(memory_space=pltpu.SMEM),
            pl.BlockSpec(memory_space=pltpu.HBM),
        ]
        + vmem(1 + len(state)),
        out_specs=tuple(vmem(4)),
        scratch_shapes=[
            pltpu.VMEM(queries.shape, jnp.bfloat16),
            pltpu.VMEM(half.shape, half.dtype),
            pltpu.SemaphoreType.DMA,
        ],
        compiler_params=pltpu.CompilerParams(vmem_limit_bytes=20 * 2**20),
        cost_estimate=pl.CostEstimate(
            flops=4 * rows * keys * HEAD_DIM + 8 * queries.size * width,
            bytes_accessed=4 * rows * keys + out_weight.size,
            transcendentals=rows * keys,
        ),
        name="attend_rest",
    )(firsts, out_weight, other, *state)


def layer(queries, key_rows, values, doc_lengths, out_weight):
    my_index = lax.axis_index("ctx")
    head = lax.axis_index("head")
    heads = lax.axis_size("head")
    chips = lax.axis_size("ctx") // 2
    chip, core = my_index // 2, my_index % 2

    kv_width = key_rows.shape[1]
    zero = jnp.zeros((), key_rows.dtype)
    own = lax.pad(key_rows, zero, ((0, 0, 0), (0, kv_width, 0))) + lax.pad(
        values, zero, ((0, 0, 0), (kv_width, 0, 0))
    )
    own = lax.optimization_barrier(own)
    cross = lax.ppermute(own, "ctx", [(2 * c - 15, 2 * c) for c in range(8, chips)])
    back = gather_blocks(own)
    blocks = [back[i] for i in range(BACK, 0, -1)] + [own]
    joined, cross = join(blocks, cross)
    blocks = blocks + [cross]
    other = lax.ppermute(joined, "ctx", [(i, i ^ 1) for i in range(2 * chips)])

    query_first = my_index * ROWS
    ahead = jnp.arange(BACK + 1, dtype=jnp.int32) - BACK + chip
    cross_first = jnp.where(core == 0, 2 * ROWS * (chip - 8) + ROWS, -ROWS)
    local_first = jnp.concatenate(
        [2 * ROWS * ahead + ROWS * core, jnp.stack([cross_first, query_first])]
    )
    doc_lengths = pltpu.with_memory_space_constraint(doc_lengths, pltpu.HBM)
    queries = pltpu.with_memory_space_constraint(queries, pltpu.HBM)
    out_weight = pltpu.with_memory_space_constraint(out_weight, pltpu.HBM)
    near, across = head ^ 1, heads - 1 - head
    first_mate = jnp.where(core == 0, near, across)
    second_mate = jnp.where(core == 0, across, near)
    rest_first = jnp.concatenate(
        [2 * ROWS * ahead + ROWS * (1 - core), jnp.stack([query_first, head ^ 2, first_mate, second_mate, head])]
    )
    width = out_weight.shape[1] // heads

    state = attend_local(local_first, doc_lengths, queries, out_weight, blocks)
    far_part, mate_part, second_part, own_part = attend_rest(
        rest_first, out_weight, other, state, width
    )
    far_got = head_swap(far_part, 0)
    mate_got = head_swap(mate_part, 0)
    passed = (second_part + far_got.astype(jnp.float32)).astype(jnp.bfloat16)
    last_got = head_swap(passed, 1)
    return (own_part + mate_got.astype(jnp.float32) + last_got.astype(jnp.float32)).astype(
        jnp.bfloat16
    )


def solution(mesh):
    return jax.shard_map(
        layer,
        mesh=mesh,
        in_specs=(
            P(("batch", "ctx"), "head"),
            P(("batch", "ctx"), "head"),
            P(("batch", "ctx"), "head"),
            P("batch"),
            P("head", None),
        ),
        out_specs=P(("batch", "ctx"), "head"),
        check_vma=False,
    )
```

time: 254 us -> 85.3 us (0.34)
  the two profiles are of different devices: /device:TPU:16 before, /device:TPU:390 now
where the time goes in v2:
time: 85.3 us; the launch traced here: 84.9 us
  starting transfers between devices  48.6 us (57%)
  waiting for transfers between devices  25.2 us (30%)
  Pallas kernels  8.77 us (10%)
  other arithmetic  1.89 us (2%)
    ppermute x9, starting transfers between devices, chip_send(): return lax.ppermute(value, 'ctx', pairs)  30.1 us
    ppermute x3, waiting for transfers between devices, head_swap(): return lax.ppermute(value, ('ctx', 'head'), pairs)  17.9 us
    ppermute x3, starting transfers between devices, head_swap(): return lax.ppermute(value, ('ctx', 'head'), pairs)  8.66 us
    ppermute x1, starting transfers between devices, layer(): other = lax.ppermute(joined, 'ctx', [(i, i ^ 1) for i in range(2 * chips)])  8.52 us
    pallas_call x1, Pallas kernels, attend_rest(): pl.pallas_call(rest_kernel, out_shape=tuple((jax.ShapeDtypeStruct((querie...  4.4 us
    ppermute x9, waiting for transfers between devices, chip_send(): return lax.ppermute(value, 'ctx', pairs)  4.33 us
    pallas_call x1, Pallas kernels, attend_local(): pl.pallas_call(local_kernel, out_shape=(state,) * 3 + (jax.ShapeDtypeStru...  4.29 us
    ppermute x1, waiting for transfers between devices, layer(): lax.ppermute(own, 'ctx', [(2 * c - 15, 2 * c) for c in range(8, chips)])  2.98 us
  transfers between devices with their start and end apart: 14, of which 6 were waited for; matrix products, arithmetic and copies ran while one was open for 0% of the time, Pallas kernels for 5%

profile of v2, /device:TPU:390, one launch (start us, length us, event | category | flops | bytes accessed | tf_op | source)
XLA Modules:
  0.0 84.9 jit_solution(10960191262792022945)
XLA Ops:
  0.0 0.9 %pad_add_fusion.refs_7_ = bf16[128,512]{1,0:T(8,128)(2,1)S(1)} fusion(bf16[128,256]{1,0:T(8,128)(2,1)} %param.7, bf16[128,256]{1,0:T(8,128)(2,1)} %param.6), kind=kLoop, calls=%fused_computation.2 | loop fusion | flops 262144 | bytes 262144 | tf_op jit(solution)/shard_map/add | solution.py:277
  0.9 3.6 %collective-permute-start.5 = (bf16[128,512]{1,0:T(8,128)(2,1)S(1)}, bf16[128,512]{1,0:T(8,128)(2,1)S(1)}, u32[]{:S(2)}, u32[]{:S(2)}) collective-permute-start(bf16[128,512]{1,0:T(8,128)(2,1)S(1)} %pad_add_fusion.refs_7_), channel_id=1, source_target_pairs={{0,16},{8,24},{16,32},{24,40},{32,48},{40,56},{48,64},{56,72},{64,... | collective-permute-start | bytes 393224 | tf_op jit(solution)/shard_map/ppermute | solution.py:26
  4.5 7.4 %collective-permute-start = (bf16[128,512]{1,0:T(8,128)(2,1)S(1)}, bf16[128,512]{1,0:T(8,128)(2,1)S(1)}, u32[]{:S(2)}, u32[]{:S(2)}) collective-permute-start(bf16[128,512]{1,0:T(8,128)(2,1)S(1)} %pad_add_fusion.refs_7_), channel_id=1, source_target_pairs={{0,112},{8,120},{16,128},{24,136},{32,144},{40,152},{48,160},{56,1... | collective-permute-start | bytes 393224 | tf_op jit(solution)/shard_map/ppermute | solution.py:26
  11.9 2.4 %collective-permute-start.6 = (bf16[128,512]{1,0:T(8,128)(2,1)S(1)}, bf16[128,512]{1,0:T(8,128)(2,1)S(1)}, u32[]{:S(2)}, u32[]{:S(2)}) collective-permute-start(bf16[128,512]{1,0:T(8,128)(2,1)S(1)} %collective-permute-done.5.refs_6_), channel_id=1, source_target_pairs={{16,32},{24,40},{32,48},{40,56},{48,64},{56,72},{64,80},{72,88},{8... | collective-permute-start | bytes 393224 | tf_op jit(solution)/shard_map/ppermute | solution.py:26
  14.3 0.7 collective-permute-start.2
  15.0 5.6 %collective-permute-start.1 = (bf16[128,512]{1,0:T(8,128)(2,1)S(1)}, bf16[128,512]{1,0:T(8,128)(2,1)S(1)}, u32[]{:S(2)}, u32[]{:S(2)}) collective-permute-start(bf16[128,512]{1,0:T(8,128)(2,1)S(1)} %collective-permute-done.refs_0_), channel_id=1, source_target_pairs={{112,96},{120,104},{128,112},{136,120},{144,128},{152,136},{160,14... | collective-permute-start | bytes 393224 | tf_op jit(solution)/shard_map/ppermute | solution.py:26
  20.5 0.3 collective-permute-done.6.refs_5_
  20.9 1.9 %collective-permute-start.7 = (bf16[128,512]{1,0:T(8,128)(2,1)S(1)}, bf16[128,512]{1,0:T(8,128)(2,1)S(1)}, u32[]{:S(2)}, u32[]{:S(2)}) collective-permute-start(bf16[128,512]{1,0:T(8,128)(2,1)S(1)} %collective-permute-done.6.refs_5_), channel_id=1, source_target_pairs={{32,48},{40,56},{48,64},{56,72},{64,80},{72,88},{80,96},{88,104},{... | collective-permute-start | bytes 393224 | tf_op jit(solution)/shard_map/ppermute | solution.py:26
  22.8 0.7 collective-permute-start.4
  23.5 6.0 %collective-permute-start.3 = (bf16[128,512]{1,0:T(8,128)(2,1)S(1)}, bf16[128,512]{1,0:T(8,128)(2,1)S(1)}, u32[]{:S(2)}, u32[]{:S(2)}) collective-permute-start(bf16[128,512]{1,0:T(8,128)(2,1)S(1)} %add.56.refs_1_), channel_id=1, source_target_pairs={{96,80},{104,88},{112,96},{120,104},{128,112},{136,120},{144,128},... | collective-permute-start | bytes 393224 | tf_op jit(solution)/shard_map/ppermute | solution.py:26
  29.6 1.3 %collective-permute-start.9 = (bf16[128,512]{1,0:T(8,128)(2,1)S(1)}, bf16[128,512]{1,0:T(8,128)(2,1)S(1)}, u32[]{:S(2)}, u32[]{:S(2)}) collective-permute-start(bf16[128,512]{1,0:T(8,128)(2,1)S(1)} %pad_add_fusion.refs_7_), channel_id=1, source_target_pairs={{8,128},{24,144},{40,160},{56,176},{72,192},{88,208},{104,224},{12... | collective-permute-start | bytes 393224 | tf_op jit(solution)/shard_map/ppermute | solution.py:281
  30.9 1.9 %collective-permute-start.8 = (bf16[128,512]{1,0:T(8,128)(2,1)S(1)}, bf16[128,512]{1,0:T(8,128)(2,1)S(1)}, u32[]{:S(2)}, u32[]{:S(2)}) collective-permute-start(bf16[128,512]{1,0:T(8,128)(2,1)S(1)} %collective-permute-done.7.refs_4_), channel_id=1, source_target_pairs={{48,64},{56,72},{64,80},{72,88},{80,96},{88,104},{96,112},{104,120... | collective-permute-start | bytes 393224 | tf_op jit(solution)/shard_map/ppermute | solution.py:26
  32.9 3.0 %collective-permute-done.9.refs_8_ = bf16[128,512]{1,0:T(8,128)(2,1)S(1)} collective-permute-done((bf16[128,512]{1,0:T(8,128)(2,1)S(1)}, bf16[128,512]{1,0:T(8,128)(2,1)S(1)}, u32[]{:S(2)}, u32[]{:S(2)}) %collective-permute-start.9) | collective-permute-done | bytes 131104 | tf_op jit(solution)/shard_map/ppermute | solution.py:281
  35.8 4.0 %collective-permute-done.8.refs_3_ = bf16[128,512]{1,0:T(8,128)(2,1)S(1)} collective-permute-done((bf16[128,512]{1,0:T(8,128)(2,1)S(1)}, bf16[128,512]{1,0:T(8,128)(2,1)S(1)}, u32[]{:S(2)}, u32[]{:S(2)}) %collective-permute-start.8) | collective-permute-done | bytes 131104 | tf_op jit(solution)/shard_map/ppermute | solution.py:26
  39.9 8.5 %collective-permute-start.10 = (bf16[1024,512]{1,0:T(8,128)(2,1)S(1)}, bf16[1024,512]{1,0:T(8,128)(2,1)S(1)}, u32[]{:S(2)}, u32[]{:S(2)}) collective-permute-start(bf16[1024,512]{1,0:T(8,128)(2,1)S(1)} %get-tuple-element.17), channel_id=1, source_target_pairs={{0,8},{8,0},{16,24},{24,16},{32,40},{40,32},{48,56},{56,48},{64,72... | collective-permute-start | bytes 3145736 | tf_op jit(solution)/shard_map/ppermute | solution.py:286
  48.7 4.3 %attend_local.1 = (f32[1024,128]{1,0:T(8,128)S(1)}, f32[1024,128]{1,0:T(8,128)S(1)}, f32[1024,128]{1,0:T(8,128)S(1)}, s32[128,128]{1,0:T(8,128)S(1)}, bf16[128,1...) custom-call(s32[10]{0:T(128)S(1)} %pad_add_fusion.1.first_ref, s32[64]{0:T(128)} %length_ref.1, ...), custom_call_target="tpu_custom_call" | custom-call | flops 603979776 | bytes 4718592 | tf_op jit(solution)/shard_map/attend_local/pallas_call | solution.py:215
  53.0 4.4 %attend_rest.1 = (bf16[128,1024]{1,0:T(8,128)(2,1)S(1)}, bf16[128,1024]{1,0:T(8,128)(2,1)S(1)}, f32[128,1024]{1,0:T(8,128)S(1)}, f32[128,1024]{1,0:T(8,128)S(1)}) custom-call(s32[13]{0:T(128)S(1)} %concatenate.6.first_ref, bf16[1024,4096]{1,0:T(8,128)(2,1)} %w_hbm.3, bf16[1024,512]{1,0:T(8,128)(2,1)S(1)} %collective-permute-done.10.other_ref, ...), custom_call_target="tpu_custom_call" | custom-call | flops 1610612736 | bytes 8388608 | tf_op jit(solution)/shard_map/attend_rest/pallas_call | solution.py:244
  57.4 2.4 %collective-permute-start.12 = (bf16[128,1024]{1,0:T(8,128)(2,1)S(1)}, bf16[128,1024]{1,0:T(8,128)(2,1)S(1)}, u32[]{:S(2)}, u32[]{:S(2)}) collective-permute-start(bf16[128,1024]{1,0:T(8,128)(2,1)S(1)} %get-tuple-element.28), channel_id=1, source_target_pairs={{0,2},{2,0},{4,6},{6,4},{8,14},{10,12},{12,10},{14,8},{16,18},{18,... | collective-permute-start | bytes 786440 | tf_op jit(solution)/shard_map/ppermute | solution.py:51
  59.8 4.3 %collective-permute-start.11 = (bf16[128,1024]{1,0:T(8,128)(2,1)S(1)}, bf16[128,1024]{1,0:T(8,128)(2,1)S(1)}, u32[]{:S(2)}, u32[]{:S(2)}) collective-permute-start(bf16[128,1024]{1,0:T(8,128)(2,1)S(1)} %get-tuple-element.26), channel_id=1, source_target_pairs={{0,2},{2,0},{4,6},{6,4},{8,14},{10,12},{12,10},{14,8},{16,18},{18,... | collective-permute-start | bytes 786440 | tf_op jit(solution)/shard_map/ppermute | solution.py:51
  64.2 7.1 %collective-permute-done.12 = bf16[128,1024]{1,0:T(8,128)(2,1)S(1)} collective-permute-done((bf16[128,1024]{1,0:T(8,128)(2,1)S(1)}, bf16[128,1024]{1,0:T(8,128)(2,1)S(1)}, u32[]{:S(2)}, u32[]{:S(2)}) %collective-permute-start.12) | collective-permute-done | bytes 262176 | tf_op jit(solution)/shard_map/ppermute | solution.py:51
  71.3 1.9 %collective-permute-start.13 = (bf16[128,1024]{1,0:T(8,128)(2,1)S(1)}, bf16[128,1024]{1,0:T(8,128)(2,1)S(1)}, u32[]{:S(2)}, u32[]{:S(2)}) collective-permute-start(bf16[128,1024]{1,0:T(8,128)(2,1)S(1)} %add_convert_fusion.1), channel_id=1, source_target_pairs={{0,6},{2,4},{4,2},{6,0},{8,10},{10,8},{12,14},{14,12},{16,22},{18,... | collective-permute-start | bytes 786440 | tf_op jit(solution)/shard_map/ppermute | solution.py:51
  73.3 3.6 %collective-permute-done.11 = bf16[128,1024]{1,0:T(8,128)(2,1)S(1)} collective-permute-done((bf16[128,1024]{1,0:T(8,128)(2,1)S(1)}, bf16[128,1024]{1,0:T(8,128)(2,1)S(1)}, u32[]{:S(2)}, u32[]{:S(2)}) %collective-permute-start.11) | collective-permute-done | bytes 262176 | tf_op jit(solution)/shard_map/ppermute | solution.py:51
  76.9 7.2 %collective-permute-done.13 = bf16[128,1024]{1,0:T(8,128)(2,1)S(1)} collective-permute-done((bf16[128,1024]{1,0:T(8,128)(2,1)S(1)}, bf16[128,1024]{1,0:T(8,128)(2,1)S(1)}, u32[]{:S(2)}, u32[]{:S(2)}) %collective-permute-start.13) | collective-permute-done | bytes 262176 | tf_op jit(solution)/shard_map/ppermute | solution.py:51
  84.1 0.8 add_convert_fusion
  (16 shorter events, 0.4 us)
Async XLA Ops:
  0.9 11.0 %collective-permute-start.5 = (bf16[128,512]{1,0:T(8,128)(2,1)S(1)}, bf16[128,512]{1,0:T(8,128)(2,1)S(1)}, u32[]{:S(2)}, u32[]{:S(2)}) collective-permute-start(bf16[128,512]{1,0:T(8,128)(2,1)S(1)} %pad_add_fusion.refs_7_), channel_id=1, source_target_pairs={{0,16},{8,24},{16,32},{24,40},{32,48},{40,56},{48,64},{56,72},{64,... | collective-permute-start | bytes 393224 | tf_op jit(solution)/shard_map/ppermute | solution.py:26
  4.5 10.5 %collective-permute-start = (bf16[128,512]{1,0:T(8,128)(2,1)S(1)}, bf16[128,512]{1,0:T(8,128)(2,1)S(1)}, u32[]{:S(2)}, u32[]{:S(2)}) collective-permute-start(bf16[128,512]{1,0:T(8,128)(2,1)S(1)} %pad_add_fusion.refs_7_), channel_id=1, source_target_pairs={{0,112},{8,120},{16,128},{24,136},{32,144},{40,152},{48,160},{56,1... | collective-permute-start | bytes 393224 | tf_op jit(solution)/shard_map/ppermute | solution.py:26
  11.9 9.0 %collective-permute-start.6 = (bf16[128,512]{1,0:T(8,128)(2,1)S(1)}, bf16[128,512]{1,0:T(8,128)(2,1)S(1)}, u32[]{:S(2)}, u32[]{:S(2)}) collective-permute-start(bf16[128,512]{1,0:T(8,128)(2,1)S(1)} %collective-permute-done.5.refs_6_), channel_id=1, source_target_pairs={{16,32},{24,40},{32,48},{40,56},{48,64},{56,72},{64,80},{72,88},{8... | collective-permute-start | bytes 393224 | tf_op jit(solution)/shard_map/ppermute | solution.py:26
  14.3 9.2 %collective-permute-start.2 = (bf16[128,512]{1,0:T(8,128)(2,1)S(1)}, bf16[128,512]{1,0:T(8,128)(2,1)S(1)}, u32[]{:S(2)}, u32[]{:S(2)}) collective-permute-start(bf16[128,512]{1,0:T(8,128)(2,1)S(1)} %pad_add_fusion.refs_7_), channel_id=1, source_target_pairs={{912,1008},{920,1016},{913,1009},{921,1017},{914,1010},{922,1018},... | collective-permute-start | bytes 393224 | tf_op jit(solution)/shard_map/ppermute | solution.py:26
  15.0 8.5 %collective-permute-start.1 = (bf16[128,512]{1,0:T(8,128)(2,1)S(1)}, bf16[128,512]{1,0:T(8,128)(2,1)S(1)}, u32[]{:S(2)}, u32[]{:S(2)}) collective-permute-start(bf16[128,512]{1,0:T(8,128)(2,1)S(1)} %collective-permute-done.refs_0_), channel_id=1, source_target_pairs={{112,96},{120,104},{128,112},{136,120},{144,128},{152,136},{160,14... | collective-permute-start | bytes 393224 | tf_op jit(solution)/shard_map/ppermute | solution.py:26
  20.9 10.0 %collective-permute-start.7 = (bf16[128,512]{1,0:T(8,128)(2,1)S(1)}, bf16[128,512]{1,0:T(8,128)(2,1)S(1)}, u32[]{:S(2)}, u32[]{:S(2)}) collective-permute-start(bf16[128,512]{1,0:T(8,128)(2,1)S(1)} %collective-permute-done.6.refs_5_), channel_id=1, source_target_pairs={{32,48},{40,56},{48,64},{56,72},{64,80},{72,88},{80,96},{88,104},{... | collective-permute-start | bytes 393224 | tf_op jit(solution)/shard_map/ppermute | solution.py:26
  22.8 10.0 %collective-permute-start.4 = (bf16[128,512]{1,0:T(8,128)(2,1)S(1)}, bf16[128,512]{1,0:T(8,128)(2,1)S(1)}, u32[]{:S(2)}, u32[]{:S(2)}) collective-permute-start(bf16[128,512]{1,0:T(8,128)(2,1)S(1)} %pad_add_fusion.refs_7_), channel_id=1, source_target_pairs={{912,992},{920,1000},{928,1008},{936,1016},{913,993},{921,1001},{9... | collective-permute-start | bytes 393224 | tf_op jit(solution)/shard_map/ppermute | solution.py:26
  23.5 9.3 %collective-permute-start.3 = (bf16[128,512]{1,0:T(8,128)(2,1)S(1)}, bf16[128,512]{1,0:T(8,128)(2,1)S(1)}, u32[]{:S(2)}, u32[]{:S(2)}) collective-permute-start(bf16[128,512]{1,0:T(8,128)(2,1)S(1)} %add.56.refs_1_), channel_id=1, source_target_pairs={{96,80},{104,88},{112,96},{120,104},{128,112},{136,120},{144,128},... | collective-permute-start | bytes 393224 | tf_op jit(solution)/shard_map/ppermute | solution.py:26
  29.6 6.3 %collective-permute-start.9 = (bf16[128,512]{1,0:T(8,128)(2,1)S(1)}, bf16[128,512]{1,0:T(8,128)(2,1)S(1)}, u32[]{:S(2)}, u32[]{:S(2)}) collective-permute-start(bf16[128,512]{1,0:T(8,128)(2,1)S(1)} %pad_add_fusion.refs_7_), channel_id=1, source_target_pairs={{8,128},{24,144},{40,160},{56,176},{72,192},{88,208},{104,224},{12... | collective-permute-start | bytes 393224 | tf_op jit(solution)/shard_map/ppermute | solution.py:281
  30.9 9.0 %collective-permute-start.8 = (bf16[128,512]{1,0:T(8,128)(2,1)S(1)}, bf16[128,512]{1,0:T(8,128)(2,1)S(1)}, u32[]{:S(2)}, u32[]{:S(2)}) collective-permute-start(bf16[128,512]{1,0:T(8,128)(2,1)S(1)} %collective-permute-done.7.refs_4_), channel_id=1, source_target_pairs={{48,64},{56,72},{64,80},{72,88},{80,96},{88,104},{96,112},{104,120... | collective-permute-start | bytes 393224 | tf_op jit(solution)/shard_map/ppermute | solution.py:26
  39.9 13.1 %collective-permute-start.10 = (bf16[1024,512]{1,0:T(8,128)(2,1)S(1)}, bf16[1024,512]{1,0:T(8,128)(2,1)S(1)}, u32[]{:S(2)}, u32[]{:S(2)}) collective-permute-start(bf16[1024,512]{1,0:T(8,128)(2,1)S(1)} %get-tuple-element.17), channel_id=1, source_target_pairs={{0,8},{8,0},{16,24},{24,16},{32,40},{40,32},{48,56},{56,48},{64,72... | collective-permute-start | bytes 3145736 | tf_op jit(solution)/shard_map/ppermute | solution.py:286
  57.4 13.9 %collective-permute-start.12 = (bf16[128,1024]{1,0:T(8,128)(2,1)S(1)}, bf16[128,1024]{1,0:T(8,128)(2,1)S(1)}, u32[]{:S(2)}, u32[]{:S(2)}) collective-permute-start(bf16[128,1024]{1,0:T(8,128)(2,1)S(1)} %get-tuple-element.28), channel_id=1, source_target_pairs={{0,2},{2,0},{4,6},{6,4},{8,14},{10,12},{12,10},{14,8},{16,18},{18,... | collective-permute-start | bytes 786440 | tf_op jit(solution)/shard_map/ppermute | solution.py:51
  59.8 17.0 %collective-permute-start.11 = (bf16[128,1024]{1,0:T(8,128)(2,1)S(1)}, bf16[128,1024]{1,0:T(8,128)(2,1)S(1)}, u32[]{:S(2)}, u32[]{:S(2)}) collective-permute-start(bf16[128,1024]{1,0:T(8,128)(2,1)S(1)} %get-tuple-element.26), channel_id=1, source_target_pairs={{0,2},{2,0},{4,6},{6,4},{8,14},{10,12},{12,10},{14,8},{16,18},{18,... | collective-permute-start | bytes 786440 | tf_op jit(solution)/shard_map/ppermute | solution.py:51
  71.3 12.7 %collective-permute-start.13 = (bf16[128,1024]{1,0:T(8,128)(2,1)S(1)}, bf16[128,1024]{1,0:T(8,128)(2,1)S(1)}, u32[]{:S(2)}, u32[]{:S(2)}) collective-permute-start(bf16[128,1024]{1,0:T(8,128)(2,1)S(1)} %add_convert_fusion.1), channel_id=1, source_target_pairs={{0,6},{2,4},{4,2},{6,0},{8,10},{10,8},{12,14},{14,12},{16,22},{18,... | collective-permute-start | bytes 786440 | tf_op jit(solution)/shard_map/ppermute | solution.py:51

commit v3 on v2

--- a/solution.py
+++ b/solution.py
@@ -30,15 +30,16 @@
     chips = lax.axis_size("ctx") // 2
     back = {}
     back[1] = chip_send(own, 1, range(1, chips))
+    cross = lax.ppermute(own, "ctx", [(2 * c - 15, 2 * c) for c in range(8, chips)])
     back[7] = chip_send(own, 7, range(7, chips))
-    for step in range(2, 5):
-        back[step] = chip_send(back[step - 1], 1, range(step, chips))
-        far = 8 - step
-        if far > 4:
-            relayed = chip_send(back[far + 1], -1, range(far, chips - step + 1))
-            direct = chip_send(own, far, range(chips - step + 1, chips))
-            back[far] = relayed + direct
-    return back
+    back[2] = chip_send(back[1], 1, range(2, chips))
+    relayed = chip_send(back[7], -1, range(6, chips - 1))
+    back[6] = relayed + chip_send(own, 6, range(chips - 1, chips))
+    back[3] = chip_send(back[2], 1, range(3, chips))
+    back[4] = chip_send(back[2], 2, range(4, chips))
+    relayed = chip_send(back[6], -1, range(5, chips - 2))
+    back[5] = relayed + chip_send(own, 5, range(chips - 2, chips))
+    return back, cross
 
 
 def head_swap(value, stage):
@@ -278,8 +279,7 @@
         values, zero, ((0, 0, 0), (kv_width, 0, 0))
     )
     own = lax.optimization_barrier(own)
-    cross = lax.ppermute(own, "ctx", [(2 * c - 15, 2 * c) for c in range(8, chips)])
-    back = gather_blocks(own)
+    back, cross = gather_blocks(own)
     blocks = [back[i] for i in range(BACK, 0, -1)] + [own]
     joined, cross = join(blocks, cross)
     blocks = blocks + [cross]

time: 85.3 us -> 84.7 us (level)
  starting transfers between devices: 48.6 us -> 46.5 us
  waiting for transfers between devices: 25.2 us -> 26.7 us
    ppermute x9, waiting for transfers between devices: 4.33 us -> 8.73 us  [chip_send(): return lax.ppermute(value, 'ctx', pairs)]
    ppermute x1, waiting for transfers between devices: 2.98 us -> 0.01 us  [gather_blocks(): lax.ppermute(own, 'ctx', [(2 * c - 15, 2 * c) for c in range(8, chips)])]
    ppermute x1, starting transfers between devices: 8.52 us -> 6.96 us  [layer(): other = lax.ppermute(joined, 'ctx', [(i, i ^ 1) for i in range(2 * chips)])]
where the time goes in v3:
time: 84.7 us; the launch traced here: 84.2 us
  starting transfers between devices  46.5 us (55%)
  waiting for transfers between devices  26.7 us (32%)
  Pallas kernels  8.77 us (10%)
  other arithmetic  1.89 us (2%)
    ppermute x9, starting transfers between devices, chip_send(): return lax.ppermute(value, 'ctx', pairs)  29.6 us
    ppermute x3, waiting for transfers between devices, head_swap(): return lax.ppermute(value, ('ctx', 'head'), pairs)  17.9 us
    ppermute x9, waiting for transfers between devices, chip_send(): return lax.ppermute(value, 'ctx', pairs)  8.73 us
    ppermute x3, starting transfers between devices, head_swap(): return lax.ppermute(value, ('ctx', 'head'), pairs)  8.66 us
    ppermute x1, starting transfers between devices, layer(): other = lax.ppermute(joined, 'ctx', [(i, i ^ 1) for i in range(2 * chips)])  6.96 us
    pallas_call x1, Pallas kernels, attend_rest(): pl.pallas_call(rest_kernel, out_shape=tuple((jax.ShapeDtypeStruct((querie...  4.4 us
    pallas_call x1, Pallas kernels, attend_local(): pl.pallas_call(local_kernel, out_shape=(state,) * 3 + (jax.ShapeDtypeStru...  4.29 us
  transfers between devices with their start and end apart: 14, of which 6 were waited for; matrix products, arithmetic and copies ran while one was open for 0% of the time, Pallas kernels for 5%

profile of v3, /device:TPU:390, one launch (start us, length us, event | category | flops | bytes accessed | tf_op | source)
XLA Modules:
  0.0 84.2 jit_solution(7293476777191530737)
XLA Ops:
  0.0 0.9 %pad_add_fusion.refs_7_ = bf16[128,512]{1,0:T(8,128)(2,1)S(1)} fusion(bf16[128,256]{1,0:T(8,128)(2,1)} %param.7, bf16[128,256]{1,0:T(8,128)(2,1)} %param.6), kind=kLoop, calls=%fused_computation.2 | loop fusion | flops 262144 | bytes 262144 | tf_op jit(solution)/shard_map/add | solution.py:278
  0.9 6.2 %collective-permute-start = (bf16[128,512]{1,0:T(8,128)(2,1)S(1)}, bf16[128,512]{1,0:T(8,128)(2,1)S(1)}, u32[]{:S(2)}, u32[]{:S(2)}) collective-permute-start(bf16[128,512]{1,0:T(8,128)(2,1)S(1)} %pad_add_fusion.refs_7_), channel_id=1, source_target_pairs={{0,112},{8,120},{16,128},{24,136},{32,144},{40,152},{48,160},{56,1... | collective-permute-start | bytes 393224 | tf_op jit(solution)/shard_map/ppermute | solution.py:26
  7.1 3.6 %collective-permute-start.5 = (bf16[128,512]{1,0:T(8,128)(2,1)S(1)}, bf16[128,512]{1,0:T(8,128)(2,1)S(1)}, u32[]{:S(2)}, u32[]{:S(2)}) collective-permute-start(bf16[128,512]{1,0:T(8,128)(2,1)S(1)} %pad_add_fusion.refs_7_), channel_id=1, source_target_pairs={{0,16},{8,24},{16,32},{24,40},{32,48},{40,56},{48,64},{56,72},{64,... | collective-permute-start | bytes 393224 | tf_op jit(solution)/shard_map/ppermute | solution.py:26
  10.7 0.7 collective-permute-start.2
  11.4 4.4 %collective-permute-start.1 = (bf16[128,512]{1,0:T(8,128)(2,1)S(1)}, bf16[128,512]{1,0:T(8,128)(2,1)S(1)}, u32[]{:S(2)}, u32[]{:S(2)}) collective-permute-start(bf16[128,512]{1,0:T(8,128)(2,1)S(1)} %collective-permute-done.refs_0_), channel_id=1, source_target_pairs={{112,96},{120,104},{128,112},{136,120},{144,128},{152,136},{160,14... | collective-permute-start | bytes 393224 | tf_op jit(solution)/shard_map/ppermute | solution.py:26
  15.7 0.3 collective-permute-done.5.refs_6_
  16.0 1.9 %collective-permute-start.6 = (bf16[128,512]{1,0:T(8,128)(2,1)S(1)}, bf16[128,512]{1,0:T(8,128)(2,1)S(1)}, u32[]{:S(2)}, u32[]{:S(2)}) collective-permute-start(bf16[128,512]{1,0:T(8,128)(2,1)S(1)} %collective-permute-done.5.refs_6_), channel_id=1, source_target_pairs={{16,32},{24,40},{32,48},{40,56},{48,64},{56,72},{64,80},{72,88},{8... | collective-permute-start | bytes 393224 | tf_op jit(solution)/shard_map/ppermute | solution.py:26
  18.0 0.7 collective-permute-start.4
  18.7 6.0 %collective-permute-start.3 = (bf16[128,512]{1,0:T(8,128)(2,1)S(1)}, bf16[128,512]{1,0:T(8,128)(2,1)S(1)}, u32[]{:S(2)}, u32[]{:S(2)}) collective-permute-start(bf16[128,512]{1,0:T(8,128)(2,1)S(1)} %add.56.refs_1_), channel_id=1, source_target_pairs={{96,80},{104,88},{112,96},{120,104},{128,112},{136,120},{144,128},... | collective-permute-start | bytes 393224 | tf_op jit(solution)/shard_map/ppermute | solution.py:26
  24.7 1.3 %collective-permute-start.9 = (bf16[128,512]{1,0:T(8,128)(2,1)S(1)}, bf16[128,512]{1,0:T(8,128)(2,1)S(1)}, u32[]{:S(2)}, u32[]{:S(2)}) collective-permute-start(bf16[128,512]{1,0:T(8,128)(2,1)S(1)} %pad_add_fusion.refs_7_), channel_id=1, source_target_pairs={{8,128},{24,144},{40,160},{56,176},{72,192},{88,208},{104,224},{12... | collective-permute-start | bytes 393224 | tf_op jit(solution)/shard_map/ppermute | solution.py:33
  26.0 1.9 %collective-permute-start.8 = (bf16[128,512]{1,0:T(8,128)(2,1)S(1)}, bf16[128,512]{1,0:T(8,128)(2,1)S(1)}, u32[]{:S(2)}, u32[]{:S(2)}) collective-permute-start(bf16[128,512]{1,0:T(8,128)(2,1)S(1)} %collective-permute-done.6.refs_5_), channel_id=1, source_target_pairs={{32,48},{40,56},{48,64},{56,72},{64,80},{72,88},{80,96},{88,104},{... | collective-permute-start | bytes 393224 | tf_op jit(solution)/shard_map/ppermute | solution.py:26
  28.0 4.3 %collective-permute-start.7 = (bf16[128,512]{1,0:T(8,128)(2,1)S(1)}, bf16[128,512]{1,0:T(8,128)(2,1)S(1)}, u32[]{:S(2)}, u32[]{:S(2)}) collective-permute-start(bf16[128,512]{1,0:T(8,128)(2,1)S(1)} %collective-permute-done.6.refs_5_), channel_id=1, source_target_pairs={{32,64},{40,72},{48,80},{56,88},{64,96},{72,104},{80,112},{88,120}... | collective-permute-start | bytes 393224 | tf_op jit(solution)/shard_map/ppermute | solution.py:26
  32.3 2.7 %collective-permute-done.8.refs_4_ = bf16[128,512]{1,0:T(8,128)(2,1)S(1)} collective-permute-done((bf16[128,512]{1,0:T(8,128)(2,1)S(1)}, bf16[128,512]{1,0:T(8,128)(2,1)S(1)}, u32[]{:S(2)}, u32[]{:S(2)}) %collective-permute-start.8) | collective-permute-done | bytes 131104 | tf_op jit(solution)/shard_map/ppermute | solution.py:26
  35.0 5.7 %collective-permute-done.7.refs_3_ = bf16[128,512]{1,0:T(8,128)(2,1)S(1)} collective-permute-done((bf16[128,512]{1,0:T(8,128)(2,1)S(1)}, bf16[128,512]{1,0:T(8,128)(2,1)S(1)}, u32[]{:S(2)}, u32[]{:S(2)}) %collective-permute-start.7) | collective-permute-done | bytes 131104 | tf_op jit(solution)/shard_map/ppermute | solution.py:26
  40.8 7.0 %collective-permute-start.10 = (bf16[1024,512]{1,0:T(8,128)(2,1)S(1)}, bf16[1024,512]{1,0:T(8,128)(2,1)S(1)}, u32[]{:S(2)}, u32[]{:S(2)}) collective-permute-start(bf16[1024,512]{1,0:T(8,128)(2,1)S(1)} %get-tuple-element.17), channel_id=1, source_target_pairs={{0,8},{8,0},{16,24},{24,16},{32,40},{40,32},{48,56},{56,48},{64,72... | collective-permute-start | bytes 3145736 | tf_op jit(solution)/shard_map/ppermute | solution.py:286
  48.0 4.3 %attend_local.1 = (f32[1024,128]{1,0:T(8,128)S(1)}, f32[1024,128]{1,0:T(8,128)S(1)}, f32[1024,128]{1,0:T(8,128)S(1)}, s32[128,128]{1,0:T(8,128)S(1)}, bf16[128,1...) custom-call(s32[10]{0:T(128)S(1)} %pad_add_fusion.1.first_ref, s32[64]{0:T(128)} %length_ref.1, ...), custom_call_target="tpu_custom_call" | custom-call | flops 603979776 | bytes 4718592 | tf_op jit(solution)/shard_map/attend_local/pallas_call | solution.py:216
  52.3 4.4 %attend_rest.1 = (bf16[128,1024]{1,0:T(8,128)(2,1)S(1)}, bf16[128,1024]{1,0:T(8,128)(2,1)S(1)}, f32[128,1024]{1,0:T(8,128)S(1)}, f32[128,1024]{1,0:T(8,128)S(1)}) custom-call(s32[13]{0:T(128)S(1)} %concatenate.6.first_ref, bf16[1024,4096]{1,0:T(8,128)(2,1)} %w_hbm.3, bf16[1024,512]{1,0:T(8,128)(2,1)S(1)} %collective-permute-done.10.other_ref, ...), custom_call_target="tpu_custom_call" | custom-call | flops 1610612736 | bytes 8388608 | tf_op jit(solution)/shard_map/attend_rest/pallas_call | solution.py:245
  56.7 2.4 %collective-permute-start.12 = (bf16[128,1024]{1,0:T(8,128)(2,1)S(1)}, bf16[128,1024]{1,0:T(8,128)(2,1)S(1)}, u32[]{:S(2)}, u32[]{:S(2)}) collective-permute-start(bf16[128,1024]{1,0:T(8,128)(2,1)S(1)} %get-tuple-element.28), channel_id=1, source_target_pairs={{0,2},{2,0},{4,6},{6,4},{8,14},{10,12},{12,10},{14,8},{16,18},{18,... | collective-permute-start | bytes 786440 | tf_op jit(solution)/shard_map/ppermute | solution.py:52
  59.1 4.3 %collective-permute-start.11 = (bf16[128,1024]{1,0:T(8,128)(2,1)S(1)}, bf16[128,1024]{1,0:T(8,128)(2,1)S(1)}, u32[]{:S(2)}, u32[]{:S(2)}) collective-permute-start(bf16[128,1024]{1,0:T(8,128)(2,1)S(1)} %get-tuple-element.26), channel_id=1, source_target_pairs={{0,2},{2,0},{4,6},{6,4},{8,14},{10,12},{12,10},{14,8},{16,18},{18,... | collective-permute-start | bytes 786440 | tf_op jit(solution)/shard_map/ppermute | solution.py:52
  63.5 7.1 %collective-permute-done.12 = bf16[128,1024]{1,0:T(8,128)(2,1)S(1)} collective-permute-done((bf16[128,1024]{1,0:T(8,128)(2,1)S(1)}, bf16[128,1024]{1,0:T(8,128)(2,1)S(1)}, u32[]{:S(2)}, u32[]{:S(2)}) %collective-permute-start.12) | collective-permute-done | bytes 262176 | tf_op jit(solution)/shard_map/ppermute | solution.py:52
  70.7 1.9 %collective-permute-start.13 = (bf16[128,1024]{1,0:T(8,128)(2,1)S(1)}, bf16[128,1024]{1,0:T(8,128)(2,1)S(1)}, u32[]{:S(2)}, u32[]{:S(2)}) collective-permute-start(bf16[128,1024]{1,0:T(8,128)(2,1)S(1)} %add_convert_fusion.1), channel_id=1, source_target_pairs={{0,6},{2,4},{4,2},{6,0},{8,10},{10,8},{12,14},{14,12},{16,22},{18,... | collective-permute-start | bytes 786440 | tf_op jit(solution)/shard_map/ppermute | solution.py:52
  72.6 3.6 %collective-permute-done.11 = bf16[128,1024]{1,0:T(8,128)(2,1)S(1)} collective-permute-done((bf16[128,1024]{1,0:T(8,128)(2,1)S(1)}, bf16[128,1024]{1,0:T(8,128)(2,1)S(1)}, u32[]{:S(2)}, u32[]{:S(2)}) %collective-permute-start.11) | collective-permute-done | bytes 262176 | tf_op jit(solution)/shard_map/ppermute | solution.py:52
  76.2 7.2 %collective-permute-done.13 = bf16[128,1024]{1,0:T(8,128)(2,1)S(1)} collective-permute-done((bf16[128,1024]{1,0:T(8,128)(2,1)S(1)}, bf16[128,1024]{1,0:T(8,128)(2,1)S(1)}, u32[]{:S(2)}, u32[]{:S(2)}) %collective-permute-start.13) | collective-permute-done | bytes 262176 | tf_op jit(solution)/shard_map/ppermute | solution.py:52
  83.4 0.8 add_convert_fusion
  (16 shorter events, 0.4 us)
Async XLA Ops:
  0.9 10.5 %collective-permute-start = (bf16[128,512]{1,0:T(8,128)(2,1)S(1)}, bf16[128,512]{1,0:T(8,128)(2,1)S(1)}, u32[]{:S(2)}, u32[]{:S(2)}) collective-permute-start(bf16[128,512]{1,0:T(8,128)(2,1)S(1)} %pad_add_fusion.refs_7_), channel_id=1, source_target_pairs={{0,112},{8,120},{16,128},{24,136},{32,144},{40,152},{48,160},{56,1... | collective-permute-start | bytes 393224 | tf_op jit(solution)/shard_map/ppermute | solution.py:26
  7.1 9.0 %collective-permute-start.5 = (bf16[128,512]{1,0:T(8,128)(2,1)S(1)}, bf16[128,512]{1,0:T(8,128)(2,1)S(1)}, u32[]{:S(2)}, u32[]{:S(2)}) collective-permute-start(bf16[128,512]{1,0:T(8,128)(2,1)S(1)} %pad_add_fusion.refs_7_), channel_id=1, source_target_pairs={{0,16},{8,24},{16,32},{24,40},{32,48},{40,56},{48,64},{56,72},{64,... | collective-permute-start | bytes 393224 | tf_op jit(solution)/shard_map/ppermute | solution.py:26
  10.7 8.0 %collective-permute-start.2 = (bf16[128,512]{1,0:T(8,128)(2,1)S(1)}, bf16[128,512]{1,0:T(8,128)(2,1)S(1)}, u32[]{:S(2)}, u32[]{:S(2)}) collective-permute-start(bf16[128,512]{1,0:T(8,128)(2,1)S(1)} %pad_add_fusion.refs_7_), channel_id=1, source_target_pairs={{912,1008},{920,1016},{913,1009},{921,1017},{914,1010},{922,1018},... | collective-permute-start | bytes 393224 | tf_op jit(solution)/shard_map/ppermute | solution.py:26
  11.4 7.3 %collective-permute-start.1 = (bf16[128,512]{1,0:T(8,128)(2,1)S(1)}, bf16[128,512]{1,0:T(8,128)(2,1)S(1)}, u32[]{:S(2)}, u32[]{:S(2)}) collective-permute-start(bf16[128,512]{1,0:T(8,128)(2,1)S(1)} %collective-permute-done.refs_0_), channel_id=1, source_target_pairs={{112,96},{120,104},{128,112},{136,120},{144,128},{152,136},{160,14... | collective-permute-start | bytes 393224 | tf_op jit(solution)/shard_map/ppermute | solution.py:26
  16.0 10.0 %collective-permute-start.6 = (bf16[128,512]{1,0:T(8,128)(2,1)S(1)}, bf16[128,512]{1,0:T(8,128)(2,1)S(1)}, u32[]{:S(2)}, u32[]{:S(2)}) collective-permute-start(bf16[128,512]{1,0:T(8,128)(2,1)S(1)} %collective-permute-done.5.refs_6_), channel_id=1, source_target_pairs={{16,32},{24,40},{32,48},{40,56},{48,64},{56,72},{64,80},{72,88},{8... | collective-permute-start | bytes 393224 | tf_op jit(solution)/shard_map/ppermute | solution.py:26
  18.0 14.3 %collective-permute-start.4 = (bf16[128,512]{1,0:T(8,128)(2,1)S(1)}, bf16[128,512]{1,0:T(8,128)(2,1)S(1)}, u32[]{:S(2)}, u32[]{:S(2)}) collective-permute-start(bf16[128,512]{1,0:T(8,128)(2,1)S(1)} %pad_add_fusion.refs_7_), channel_id=1, source_target_pairs={{912,992},{920,1000},{928,1008},{936,1016},{913,993},{921,1001},{9... | collective-permute-start | bytes 393224 | tf_op jit(solution)/shard_map/ppermute | solution.py:26
  18.7 13.6 %collective-permute-start.3 = (bf16[128,512]{1,0:T(8,128)(2,1)S(1)}, bf16[128,512]{1,0:T(8,128)(2,1)S(1)}, u32[]{:S(2)}, u32[]{:S(2)}) collective-permute-start(bf16[128,512]{1,0:T(8,128)(2,1)S(1)} %add.56.refs_1_), channel_id=1, source_target_pairs={{96,80},{104,88},{112,96},{120,104},{128,112},{136,120},{144,128},... | collective-permute-start | bytes 393224 | tf_op jit(solution)/shard_map/ppermute | solution.py:26
  24.7 7.6 %collective-permute-start.9 = (bf16[128,512]{1,0:T(8,128)(2,1)S(1)}, bf16[128,512]{1,0:T(8,128)(2,1)S(1)}, u32[]{:S(2)}, u32[]{:S(2)}) collective-permute-start(bf16[128,512]{1,0:T(8,128)(2,1)S(1)} %pad_add_fusion.refs_7_), channel_id=1, source_target_pairs={{8,128},{24,144},{40,160},{56,176},{72,192},{88,208},{104,224},{12... | collective-permute-start | bytes 393224 | tf_op jit(solution)/shard_map/ppermute | solution.py:33
  26.0 9.0 %collective-permute-start.8 = (bf16[128,512]{1,0:T(8,128)(2,1)S(1)}, bf16[128,512]{1,0:T(8,128)(2,1)S(1)}, u32[]{:S(2)}, u32[]{:S(2)}) collective-permute-start(bf16[128,512]{1,0:T(8,128)(2,1)S(1)} %collective-permute-done.6.refs_5_), channel_id=1, source_target_pairs={{32,48},{40,56},{48,64},{56,72},{64,80},{72,88},{80,96},{88,104},{... | collective-permute-start | bytes 393224 | tf_op jit(solution)/shard_map/ppermute | solution.py:26
  28.0 12.8 %collective-permute-start.7 = (bf16[128,512]{1,0:T(8,128)(2,1)S(1)}, bf16[128,512]{1,0:T(8,128)(2,1)S(1)}, u32[]{:S(2)}, u32[]{:S(2)}) collective-permute-start(bf16[128,512]{1,0:T(8,128)(2,1)S(1)} %collective-permute-done.6.refs_5_), channel_id=1, source_target_pairs={{32,64},{40,72},{48,80},{56,88},{64,96},{72,104},{80,112},{88,120}... | collective-permute-start | bytes 393224 | tf_op jit(solution)/shard_map/ppermute | solution.py:26
  40.8 11.5 %collective-permute-start.10 = (bf16[1024,512]{1,0:T(8,128)(2,1)S(1)}, bf16[1024,512]{1,0:T(8,128)(2,1)S(1)}, u32[]{:S(2)}, u32[]{:S(2)}) collective-permute-start(bf16[1024,512]{1,0:T(8,128)(2,1)S(1)} %get-tuple-element.17), channel_id=1, source_target_pairs={{0,8},{8,0},{16,24},{24,16},{32,40},{40,32},{48,56},{56,48},{64,72... | collective-permute-start | bytes 3145736 | tf_op jit(solution)/shard_map/ppermute | solution.py:286
  56.7 13.9 %collective-permute-start.12 = (bf16[128,1024]{1,0:T(8,128)(2,1)S(1)}, bf16[128,1024]{1,0:T(8,128)(2,1)S(1)}, u32[]{:S(2)}, u32[]{:S(2)}) collective-permute-start(bf16[128,1024]{1,0:T(8,128)(2,1)S(1)} %get-tuple-element.28), channel_id=1, source_target_pairs={{0,2},{2,0},{4,6},{6,4},{8,14},{10,12},{12,10},{14,8},{16,18},{18,... | collective-permute-start | bytes 786440 | tf_op jit(solution)/shard_map/ppermute | solution.py:52
  59.1 17.0 %collective-permute-start.11 = (bf16[128,1024]{1,0:T(8,128)(2,1)S(1)}, bf16[128,1024]{1,0:T(8,128)(2,1)S(1)}, u32[]{:S(2)}, u32[]{:S(2)}) collective-permute-start(bf16[128,1024]{1,0:T(8,128)(2,1)S(1)} %get-tuple-element.26), channel_id=1, source_target_pairs={{0,2},{2,0},{4,6},{6,4},{8,14},{10,12},{12,10},{14,8},{16,18},{18,... | collective-permute-start | bytes 786440 | tf_op jit(solution)/shard_map/ppermute | solution.py:52
  70.7 12.7 %collective-permute-start.13 = (bf16[128,1024]{1,0:T(8,128)(2,1)S(1)}, bf16[128,1024]{1,0:T(8,128)(2,1)S(1)}, u32[]{:S(2)}, u32[]{:S(2)}) collective-permute-start(bf16[128,1024]{1,0:T(8,128)(2,1)S(1)} %add_convert_fusion.1), channel_id=1, source_target_pairs={{0,6},{2,4},{4,2},{6,0},{8,10},{10,8},{12,14},{14,12},{16,22},{18,... | collective-permute-start | bytes 786440 | tf_op jit(solution)/shard_map/ppermute | solution.py:52

commit v4 on v3

--- a/solution.py
+++ b/solution.py
@@ -91,11 +91,9 @@
     return jnp.broadcast_to(starts[:1], (ROWS, ROWS)).T
 
 
-def local_kernel(first_ref, length_ref, q_hbm, w_hbm, *refs):
-    blocks, (peak_ref, total_ref, mixed_ref, start_ref, q_ref, w_ref, sems) = refs[:-7], refs[-7:]
-    fetch_q = pltpu.make_async_copy(q_hbm, q_ref, sems.at[0])
-    fetch_w = pltpu.make_async_copy(w_hbm.at[: w_ref.shape[0]], w_ref, sems.at[1])
-    fetch_q.start()
+def local_kernel(first_ref, length_ref, w_hbm, q_ref, *refs):
+    blocks, (peak_ref, total_ref, mixed_ref, start_ref, w_ref, sem) = refs[:-6], refs[-6:]
+    fetch_w = pltpu.make_async_copy(w_hbm.at[: w_ref.shape[0]], w_ref, sem)
     fetch_w.start()
     start_ref[...] = document_starts(length_ref, first_ref[len(blocks)])
     kv_width = blocks[0].shape[1] // 2
@@ -103,7 +101,6 @@
         [masked_bias(first_ref[i], start_ref, first_ref[len(blocks)]) for i in range(len(blocks))],
         axis=1,
     )
-    fetch_q.wait()
     for pair in range(kv_width // HEAD_DIM):
         low, high = pair * HEAD_DIM, (pair + 1) * HEAD_DIM
         keys = jnp.concatenate([b[:, low:high] for b in blocks], axis=0)
@@ -218,14 +215,13 @@
         out_shape=(state,) * 3
         + (
             jax.ShapeDtypeStruct((ROWS, ROWS), jnp.int32),
-            jax.ShapeDtypeStruct(queries.shape, queries.dtype),
             half_weight(out_weight),
         ),
         in_specs=[pl.BlockSpec(memory_space=pltpu.SMEM)] * 2
-        + [pl.BlockSpec(memory_space=pltpu.HBM)] * 2
-        + vmem(len(blocks)),
-        out_specs=tuple(vmem(6)),
-        scratch_shapes=[pltpu.SemaphoreType.DMA((2,))],
+        + [pl.BlockSpec(memory_space=pltpu.HBM)]
+        + vmem(1 + len(blocks)),
+        out_specs=tuple(vmem(5)),
+        scratch_shapes=[pltpu.SemaphoreType.DMA],
         compiler_params=pltpu.CompilerParams(vmem_limit_bytes=16 * 2**20),
         cost_estimate=pl.CostEstimate(
             flops=4 * rows * keys * HEAD_DIM,
@@ -233,7 +229,7 @@
             transcendentals=rows * keys,
         ),
         name="attend_local",
-    )(firsts, doc_lengths, queries, out_weight, *blocks)
+    )(firsts, doc_lengths, out_weight, queries, *blocks)
 
 
 def attend_rest(firsts, out_weight, other, state, width):
@@ -292,7 +288,7 @@
         [2 * ROWS * ahead + ROWS * core, jnp.stack([cross_first, query_first])]
     )
     doc_lengths = pltpu.with_memory_space_constraint(doc_lengths, pltpu.HBM)
-    queries = pltpu.with_memory_space_constraint(queries, pltpu.HBM)
+    queries = queries * (my_index >= 0).astype(queries.dtype)
     out_weight = pltpu.with_memory_space_constraint(out_weight, pltpu.HBM)
     near, across = head ^ 1, heads - 1 - head
     first_mate = jnp.where(core == 0, near, across)
@@ -302,7 +298,8 @@
     )
     width = out_weight.shape[1] // heads
 
-    state = attend_local(local_first, doc_lengths, queries, out_weight, blocks)
+    *state, half = attend_local(local_first, doc_lengths, queries, out_weight, blocks)
+    state = (*state, queries, half)
     far_part, mate_part, second_part, own_part = attend_rest(
         rest_first, out_weight, other, state, width
     )

time: 84.7 us -> 84.8 us (level)
  other arithmetic: 1.89 us -> 2.89 us
  Pallas kernels: 8.77 us -> 7.85 us
    mul x0 -> x1, other arithmetic: none -> 0.97 us  [layer(): queries = queries * (my_index >= 0).astype(queries.dtype)]
    pallas_call x1, Pallas kernels: 4.29 us -> 3.37 us  [attend_local(): pl.pallas_call(local_kernel, out_shape=(state,) * 3 + (jax.ShapeDtypeStru...]
  transfers between devices with their start and end apart: 14 -> 14, of which waited for: 6 -> 6; matrix products, arithmetic and copies ran while one was open for 0% -> 2% of each run, Pallas kernels for 5% -> 4%
where the time goes in v4:
time: 84.8 us; the launch traced here: 84.2 us
  starting transfers between devices  46.5 us (55%)
  waiting for transfers between devices  26.6 us (31%)
  Pallas kernels  7.85 us (9%)
  other arithmetic  2.89 us (3%)
    ppermute x9, starting transfers between devices, chip_send(): return lax.ppermute(value, 'ctx', pairs)  29.6 us
    ppermute x3, waiting for transfers between devices, head_swap(): return lax.ppermute(value, ('ctx', 'head'), pairs)  17.9 us
    ppermute x9, waiting for transfers between devices, chip_send(): return lax.ppermute(value, 'ctx', pairs)  8.73 us
    ppermute x3, starting transfers between devices, head_swap(): return lax.ppermute(value, ('ctx', 'head'), pairs)  8.66 us
    ppermute x1, starting transfers between devices, layer(): other = lax.ppermute(joined, 'ctx', [(i, i ^ 1) for i in range(2 * chips)])  6.96 us
    pallas_call x1, Pallas kernels, attend_rest(): pl.pallas_call(rest_kernel, out_shape=tuple((jax.ShapeDtypeStruct((querie...  4.4 us
    pallas_call x1, Pallas kernels, attend_local(): pl.pallas_call(local_kernel, out_shape=(state,) * 3 + (jax.ShapeDtypeStru...  3.37 us
  transfers between devices with their start and end apart: 14, of which 6 were waited for; matrix products, arithmetic and copies ran while one was open for 2% of the time, Pallas kernels for 4%

profile of v4, /device:TPU:390, one launch (start us, length us, event | category | flops | bytes accessed | tf_op | source)
XLA Modules:
  0.0 84.2 jit_solution(5571259724018425063)
XLA Ops:
  0.0 0.9 %pad_add_fusion.refs_7_ = bf16[128,512]{1,0:T(8,128)(2,1)S(1)} fusion(bf16[128,256]{1,0:T(8,128)(2,1)} %param.7, bf16[128,256]{1,0:T(8,128)(2,1)} %param.6), kind=kLoop, calls=%fused_computation.3 | loop fusion | flops 262144 | bytes 262144 | tf_op jit(solution)/shard_map/add | solution.py:274
  0.9 6.2 %collective-permute-start = (bf16[128,512]{1,0:T(8,128)(2,1)S(1)}, bf16[128,512]{1,0:T(8,128)(2,1)S(1)}, u32[]{:S(2)}, u32[]{:S(2)}) collective-permute-start(bf16[128,512]{1,0:T(8,128)(2,1)S(1)} %pad_add_fusion.refs_7_), channel_id=1, source_target_pairs={{0,112},{8,120},{16,128},{24,136},{32,144},{40,152},{48,160},{56,1... | collective-permute-start | bytes 393224 | tf_op jit(solution)/shard_map/ppermute | solution.py:26
  7.1 3.6 %collective-permute-start.5 = (bf16[128,512]{1,0:T(8,128)(2,1)S(1)}, bf16[128,512]{1,0:T(8,128)(2,1)S(1)}, u32[]{:S(2)}, u32[]{:S(2)}) collective-permute-start(bf16[128,512]{1,0:T(8,128)(2,1)S(1)} %pad_add_fusion.refs_7_), channel_id=1, source_target_pairs={{0,16},{8,24},{16,32},{24,40},{32,48},{40,56},{48,64},{56,72},{64,... | collective-permute-start | bytes 393224 | tf_op jit(solution)/shard_map/ppermute | solution.py:26
  10.7 0.7 collective-permute-start.2
  11.4 4.4 %collective-permute-start.1 = (bf16[128,512]{1,0:T(8,128)(2,1)S(1)}, bf16[128,512]{1,0:T(8,128)(2,1)S(1)}, u32[]{:S(2)}, u32[]{:S(2)}) collective-permute-start(bf16[128,512]{1,0:T(8,128)(2,1)S(1)} %collective-permute-done.refs_0_), channel_id=1, source_target_pairs={{112,96},{120,104},{128,112},{136,120},{144,128},{152,136},{160,14... | collective-permute-start | bytes 393224 | tf_op jit(solution)/shard_map/ppermute | solution.py:26
  16.0 1.9 %collective-permute-start.6 = (bf16[128,512]{1,0:T(8,128)(2,1)S(1)}, bf16[128,512]{1,0:T(8,128)(2,1)S(1)}, u32[]{:S(2)}, u32[]{:S(2)}) collective-permute-start(bf16[128,512]{1,0:T(8,128)(2,1)S(1)} %collective-permute-done.5.refs_6_), channel_id=1, source_target_pairs={{16,32},{24,40},{32,48},{40,56},{48,64},{56,72},{64,80},{72,88},{8... | collective-permute-start | bytes 393224 | tf_op jit(solution)/shard_map/ppermute | solution.py:26
  18.0 0.7 collective-permute-start.4
  18.7 6.0 %collective-permute-start.3 = (bf16[128,512]{1,0:T(8,128)(2,1)S(1)}, bf16[128,512]{1,0:T(8,128)(2,1)S(1)}, u32[]{:S(2)}, u32[]{:S(2)}) collective-permute-start(bf16[128,512]{1,0:T(8,128)(2,1)S(1)} %add.56.refs_1_), channel_id=1, source_target_pairs={{96,80},{104,88},{112,96},{120,104},{128,112},{136,120},{144,128},... | collective-permute-start | bytes 393224 | tf_op jit(solution)/shard_map/ppermute | solution.py:26
  24.7 1.3 %collective-permute-start.9 = (bf16[128,512]{1,0:T(8,128)(2,1)S(1)}, bf16[128,512]{1,0:T(8,128)(2,1)S(1)}, u32[]{:S(2)}, u32[]{:S(2)}) collective-permute-start(bf16[128,512]{1,0:T(8,128)(2,1)S(1)} %pad_add_fusion.refs_7_), channel_id=1, source_target_pairs={{8,128},{24,144},{40,160},{56,176},{72,192},{88,208},{104,224},{12... | collective-permute-start | bytes 393224 | tf_op jit(solution)/shard_map/ppermute | solution.py:33
  26.0 1.9 %collective-permute-start.8 = (bf16[128,512]{1,0:T(8,128)(2,1)S(1)}, bf16[128,512]{1,0:T(8,128)(2,1)S(1)}, u32[]{:S(2)}, u32[]{:S(2)}) collective-permute-start(bf16[128,512]{1,0:T(8,128)(2,1)S(1)} %collective-permute-done.6.refs_5_), channel_id=1, source_target_pairs={{32,48},{40,56},{48,64},{56,72},{64,80},{72,88},{80,96},{88,104},{... | collective-permute-start | bytes 393224 | tf_op jit(solution)/shard_map/ppermute | solution.py:26
  28.0 4.3 %collective-permute-start.7 = (bf16[128,512]{1,0:T(8,128)(2,1)S(1)}, bf16[128,512]{1,0:T(8,128)(2,1)S(1)}, u32[]{:S(2)}, u32[]{:S(2)}) collective-permute-start(bf16[128,512]{1,0:T(8,128)(2,1)S(1)} %collective-permute-done.6.refs_5_), channel_id=1, source_target_pairs={{32,64},{40,72},{48,80},{56,88},{64,96},{72,104},{80,112},{88,120}... | collective-permute-start | bytes 393224 | tf_op jit(solution)/shard_map/ppermute | solution.py:26
  32.3 2.7 %collective-permute-done.8.refs_4_ = bf16[128,512]{1,0:T(8,128)(2,1)S(1)} collective-permute-done((bf16[128,512]{1,0:T(8,128)(2,1)S(1)}, bf16[128,512]{1,0:T(8,128)(2,1)S(1)}, u32[]{:S(2)}, u32[]{:S(2)}) %collective-permute-start.8) | collective-permute-done | bytes 131104 | tf_op jit(solution)/shard_map/ppermute | solution.py:26
  35.0 5.7 %collective-permute-done.7.refs_3_ = bf16[128,512]{1,0:T(8,128)(2,1)S(1)} collective-permute-done((bf16[128,512]{1,0:T(8,128)(2,1)S(1)}, bf16[128,512]{1,0:T(8,128)(2,1)S(1)}, u32[]{:S(2)}, u32[]{:S(2)}) %collective-permute-start.7) | collective-permute-done | bytes 131104 | tf_op jit(solution)/shard_map/ppermute | solution.py:26
  40.8 7.0 %collective-permute-start.10 = (bf16[1024,512]{1,0:T(8,128)(2,1)S(1)}, bf16[1024,512]{1,0:T(8,128)(2,1)S(1)}, u32[]{:S(2)}, u32[]{:S(2)}) collective-permute-start(bf16[1024,512]{1,0:T(8,128)(2,1)S(1)} %get-tuple-element.16), channel_id=1, source_target_pairs={{0,8},{8,0},{16,24},{24,16},{32,40},{40,32},{48,56},{56,48},{64,72... | collective-permute-start | bytes 3145736 | tf_op jit(solution)/shard_map/ppermute | solution.py:282
  48.0 1.0 %broadcast_multiply_fusion.q_ref = bf16[128,1024]{1,0:T(8,128)(2,1)S(1)} fusion(bf16[128,1024]{1,0:T(8,128)(2,1)} %param.5, bf16[]{:T(256)S(6)} %convert_element_type.18), kind=kLoop, calls=%fused_computation.2 | loop fusion | flops 131072 | bytes 524290 | tf_op jit(solution)/shard_map/mul | solution.py:291
  49.0 3.4 %attend_local.1 = (f32[1024,128]{1,0:T(8,128)S(1)}, f32[1024,128]{1,0:T(8,128)S(1)}, f32[1024,128]{1,0:T(8,128)S(1)}, s32[128,128]{1,0:T(8,128)S(1)}, bf16[512,4096]{1,0:T(8,128)(2,1)S(1)}) custom-call(s32[10]{0:T(128)S(1)} %pad_add_fusion.1.first_ref, s32[64]{0:T(128)} %length_ref.1, bf16[1024,4096]{1,0:T(8,128)(2,1)} %w_hbm.3, ...), custom_call_target="tpu_custom_call" | custom-call | flops 603979776 | bytes 4718592 | tf_op jit(solution)/shard_map/attend_local/pallas_call | solution.py:213
  52.4 4.4 %attend_rest.1 = (bf16[128,1024]{1,0:T(8,128)(2,1)S(1)}, bf16[128,1024]{1,0:T(8,128)(2,1)S(1)}, f32[128,1024]{1,0:T(8,128)S(1)}, f32[128,1024]{1,0:T(8,128)S(1)}) custom-call(s32[13]{0:T(128)S(1)} %concatenate.6.first_ref, bf16[1024,4096]{1,0:T(8,128)(2,1)} %w_hbm.3, bf16[1024,512]{1,0:T(8,128)(2,1)S(1)} %collective-permute-done.10.other_ref, ...), custom_call_target="tpu_custom_call" | custom-call | flops 1610612736 | bytes 8388608 | tf_op jit(solution)/shard_map/attend_rest/pallas_call | solution.py:241
  56.8 2.4 %collective-permute-start.12 = (bf16[128,1024]{1,0:T(8,128)(2,1)S(1)}, bf16[128,1024]{1,0:T(8,128)(2,1)S(1)}, u32[]{:S(2)}, u32[]{:S(2)}) collective-permute-start(bf16[128,1024]{1,0:T(8,128)(2,1)S(1)} %get-tuple-element.26), channel_id=1, source_target_pairs={{0,2},{2,0},{4,6},{6,4},{8,14},{10,12},{12,10},{14,8},{16,18},{18,... | collective-permute-start | bytes 786440 | tf_op jit(solution)/shard_map/ppermute | solution.py:52
  59.2 4.3 %collective-permute-start.11 = (bf16[128,1024]{1,0:T(8,128)(2,1)S(1)}, bf16[128,1024]{1,0:T(8,128)(2,1)S(1)}, u32[]{:S(2)}, u32[]{:S(2)}) collective-permute-start(bf16[128,1024]{1,0:T(8,128)(2,1)S(1)} %get-tuple-element.24), channel_id=1, source_target_pairs={{0,2},{2,0},{4,6},{6,4},{8,14},{10,12},{12,10},{14,8},{16,18},{18,... | collective-permute-start | bytes 786440 | tf_op jit(solution)/shard_map/ppermute | solution.py:52
  63.5 7.1 %collective-permute-done.12 = bf16[128,1024]{1,0:T(8,128)(2,1)S(1)} collective-permute-done((bf16[128,1024]{1,0:T(8,128)(2,1)S(1)}, bf16[128,1024]{1,0:T(8,128)(2,1)S(1)}, u32[]{:S(2)}, u32[]{:S(2)}) %collective-permute-start.12) | collective-permute-done | bytes 262176 | tf_op jit(solution)/shard_map/ppermute | solution.py:52
  70.7 1.9 %collective-permute-start.13 = (bf16[128,1024]{1,0:T(8,128)(2,1)S(1)}, bf16[128,1024]{1,0:T(8,128)(2,1)S(1)}, u32[]{:S(2)}, u32[]{:S(2)}) collective-permute-start(bf16[128,1024]{1,0:T(8,128)(2,1)S(1)} %add_convert_fusion.1), channel_id=1, source_target_pairs={{0,6},{2,4},{4,2},{6,0},{8,10},{10,8},{12,14},{14,12},{16,22},{18,... | collective-permute-start | bytes 786440 | tf_op jit(solution)/shard_map/ppermute | solution.py:52
  72.7 3.6 %collective-permute-done.11 = bf16[128,1024]{1,0:T(8,128)(2,1)S(1)} collective-permute-done((bf16[128,1024]{1,0:T(8,128)(2,1)S(1)}, bf16[128,1024]{1,0:T(8,128)(2,1)S(1)}, u32[]{:S(2)}, u32[]{:S(2)}) %collective-permute-start.11) | collective-permute-done | bytes 262176 | tf_op jit(solution)/shard_map/ppermute | solution.py:52
  76.3 7.1 %collective-permute-done.13 = bf16[128,1024]{1,0:T(8,128)(2,1)S(1)} collective-permute-done((bf16[128,1024]{1,0:T(8,128)(2,1)S(1)}, bf16[128,1024]{1,0:T(8,128)(2,1)S(1)}, u32[]{:S(2)}, u32[]{:S(2)}) %collective-permute-start.13) | collective-permute-done | bytes 262176 | tf_op jit(solution)/shard_map/ppermute | solution.py:52
  83.4 0.8 add_convert_fusion
  (17 shorter events, 0.7 us)
Async XLA Ops:
  0.9 10.5 %collective-permute-start = (bf16[128,512]{1,0:T(8,128)(2,1)S(1)}, bf16[128,512]{1,0:T(8,128)(2,1)S(1)}, u32[]{:S(2)}, u32[]{:S(2)}) collective-permute-start(bf16[128,512]{1,0:T(8,128)(2,1)S(1)} %pad_add_fusion.refs_7_), channel_id=1, source_target_pairs={{0,112},{8,120},{16,128},{24,136},{32,144},{40,152},{48,160},{56,1... | collective-permute-start | bytes 393224 | tf_op jit(solution)/shard_map/ppermute | solution.py:26
  7.1 9.0 %collective-permute-start.5 = (bf16[128,512]{1,0:T(8,128)(2,1)S(1)}, bf16[128,512]{1,0:T(8,128)(2,1)S(1)}, u32[]{:S(2)}, u32[]{:S(2)}) collective-permute-start(bf16[128,512]{1,0:T(8,128)(2,1)S(1)} %pad_add_fusion.refs_7_), channel_id=1, source_target_pairs={{0,16},{8,24},{16,32},{24,40},{32,48},{40,56},{48,64},{56,72},{64,... | collective-permute-start | bytes 393224 | tf_op jit(solution)/shard_map/ppermute | solution.py:26
  10.7 8.0 %collective-permute-start.2 = (bf16[128,512]{1,0:T(8,128)(2,1)S(1)}, bf16[128,512]{1,0:T(8,128)(2,1)S(1)}, u32[]{:S(2)}, u32[]{:S(2)}) collective-permute-start(bf16[128,512]{1,0:T(8,128)(2,1)S(1)} %pad_add_fusion.refs_7_), channel_id=1, source_target_pairs={{912,1008},{920,1016},{913,1009},{921,1017},{914,1010},{922,1018},... | collective-permute-start | bytes 393224 | tf_op jit(solution)/shard_map/ppermute | solution.py:26
  11.4 7.3 %collective-permute-start.1 = (bf16[128,512]{1,0:T(8,128)(2,1)S(1)}, bf16[128,512]{1,0:T(8,128)(2,1)S(1)}, u32[]{:S(2)}, u32[]{:S(2)}) collective-permute-start(bf16[128,512]{1,0:T(8,128)(2,1)S(1)} %collective-permute-done.refs_0_), channel_id=1, source_target_pairs={{112,96},{120,104},{128,112},{136,120},{144,128},{152,136},{160,14... | collective-permute-start | bytes 393224 | tf_op jit(solution)/shard_map/ppermute | solution.py:26
  16.0 10.0 %collective-permute-start.6 = (bf16[128,512]{1,0:T(8,128)(2,1)S(1)}, bf16[128,512]{1,0:T(8,128)(2,1)S(1)}, u32[]{:S(2)}, u32[]{:S(2)}) collective-permute-start(bf16[128,512]{1,0:T(8,128)(2,1)S(1)} %collective-permute-done.5.refs_6_), channel_id=1, source_target_pairs={{16,32},{24,40},{32,48},{40,56},{48,64},{56,72},{64,80},{72,88},{8... | collective-permute-start | bytes 393224 | tf_op jit(solution)/shard_map/ppermute | solution.py:26
  18.0 14.3 %collective-permute-start.4 = (bf16[128,512]{1,0:T(8,128)(2,1)S(1)}, bf16[128,512]{1,0:T(8,128)(2,1)S(1)}, u32[]{:S(2)}, u32[]{:S(2)}) collective-permute-start(bf16[128,512]{1,0:T(8,128)(2,1)S(1)} %pad_add_fusion.refs_7_), channel_id=1, source_target_pairs={{912,992},{920,1000},{928,1008},{936,1016},{913,993},{921,1001},{9... | collective-permute-start | bytes 393224 | tf_op jit(solution)/shard_map/ppermute | solution.py:26
  18.7 13.6 %collective-permute-start.3 = (bf16[128,512]{1,0:T(8,128)(2,1)S(1)}, bf16[128,512]{1,0:T(8,128)(2,1)S(1)}, u32[]{:S(2)}, u32[]{:S(2)}) collective-permute-start(bf16[128,512]{1,0:T(8,128)(2,1)S(1)} %add.56.refs_1_), channel_id=1, source_target_pairs={{96,80},{104,88},{112,96},{120,104},{128,112},{136,120},{144,128},... | collective-permute-start | bytes 393224 | tf_op jit(solution)/shard_map/ppermute | solution.py:26
  24.7 7.6 %collective-permute-start.9 = (bf16[128,512]{1,0:T(8,128)(2,1)S(1)}, bf16[128,512]{1,0:T(8,128)(2,1)S(1)}, u32[]{:S(2)}, u32[]{:S(2)}) collective-permute-start(bf16[128,512]{1,0:T(8,128)(2,1)S(1)} %pad_add_fusion.refs_7_), channel_id=1, source_target_pairs={{8,128},{24,144},{40,160},{56,176},{72,192},{88,208},{104,224},{12... | collective-permute-start | bytes 393224 | tf_op jit(solution)/shard_map/ppermute | solution.py:33
  26.0 9.0 %collective-permute-start.8 = (bf16[128,512]{1,0:T(8,128)(2,1)S(1)}, bf16[128,512]{1,0:T(8,128)(2,1)S(1)}, u32[]{:S(2)}, u32[]{:S(2)}) collective-permute-start(bf16[128,512]{1,0:T(8,128)(2,1)S(1)} %collective-permute-done.6.refs_5_), channel_id=1, source_target_pairs={{32,48},{40,56},{48,64},{56,72},{64,80},{72,88},{80,96},{88,104},{... | collective-permute-start | bytes 393224 | tf_op jit(solution)/shard_map/ppermute | solution.py:26
  28.0 12.8 %collective-permute-start.7 = (bf16[128,512]{1,0:T(8,128)(2,1)S(1)}, bf16[128,512]{1,0:T(8,128)(2,1)S(1)}, u32[]{:S(2)}, u32[]{:S(2)}) collective-permute-start(bf16[128,512]{1,0:T(8,128)(2,1)S(1)} %collective-permute-done.6.refs_5_), channel_id=1, source_target_pairs={{32,64},{40,72},{48,80},{56,88},{64,96},{72,104},{80,112},{88,120}... | collective-permute-start | bytes 393224 | tf_op jit(solution)/shard_map/ppermute | solution.py:26
  40.8 11.6 %collective-permute-start.10 = (bf16[1024,512]{1,0:T(8,128)(2,1)S(1)}, bf16[1024,512]{1,0:T(8,128)(2,1)S(1)}, u32[]{:S(2)}, u32[]{:S(2)}) collective-permute-start(bf16[1024,512]{1,0:T(8,128)(2,1)S(1)} %get-tuple-element.16), channel_id=1, source_target_pairs={{0,8},{8,0},{16,24},{24,16},{32,40},{40,32},{48,56},{56,48},{64,72... | collective-permute-start | bytes 3145736 | tf_op jit(solution)/shard_map/ppermute | solution.py:282
  56.8 13.9 %collective-permute-start.12 = (bf16[128,1024]{1,0:T(8,128)(2,1)S(1)}, bf16[128,1024]{1,0:T(8,128)(2,1)S(1)}, u32[]{:S(2)}, u32[]{:S(2)}) collective-permute-start(bf16[128,1024]{1,0:T(8,128)(2,1)S(1)} %get-tuple-element.26), channel_id=1, source_target_pairs={{0,2},{2,0},{4,6},{6,4},{8,14},{10,12},{12,10},{14,8},{16,18},{18,... | collective-permute-start | bytes 786440 | tf_op jit(solution)/shard_map/ppermute | solution.py:52
  59.2 17.1 %collective-permute-start.11 = (bf16[128,1024]{1,0:T(8,128)(2,1)S(1)}, bf16[128,1024]{1,0:T(8,128)(2,1)S(1)}, u32[]{:S(2)}, u32[]{:S(2)}) collective-permute-start(bf16[128,1024]{1,0:T(8,128)(2,1)S(1)} %get-tuple-element.24), channel_id=1, source_target_pairs={{0,2},{2,0},{4,6},{6,4},{8,14},{10,12},{12,10},{14,8},{16,18},{18,... | collective-permute-start | bytes 786440 | tf_op jit(solution)/shard_map/ppermute | solution.py:52
  70.7 12.7 %collective-permute-start.13 = (bf16[128,1024]{1,0:T(8,128)(2,1)S(1)}, bf16[128,1024]{1,0:T(8,128)(2,1)S(1)}, u32[]{:S(2)}, u32[]{:S(2)}) collective-permute-start(bf16[128,1024]{1,0:T(8,128)(2,1)S(1)} %add_convert_fusion.1), channel_id=1, source_target_pairs={{0,6},{2,4},{4,2},{6,0},{8,10},{10,8},{12,14},{14,12},{16,22},{18,... | collective-permute-start | bytes 786440 | tf_op jit(solution)/shard_map/ppermute | solution.py:52
